TPU v7x, 128 devices: a whole 4x4x4 slice. The times are simulated.
128 devices in a mesh: member: 8 (over y_lo, z), dp: 16 (over y_hi, x, core).
Axes of the slice: x: 4, y: 4 (y_hi: 2, y_lo: 2; y = y_hi * 2 + y_lo), z: 4, core: 2. Of those that a mesh axis runs over, the one named last changes fastest.
Arguments:
- hidden: bfloat16 [8, 8192, 4096], P('member', 'dp'), may hold values from -8 to 8
- projection: bfloat16 [8, 4096, 1024], P('member', 'dp'), may hold values from -0.09375 to 0.09375
- head_weight: bfloat16 [8, 14, 1024], P('member'), may hold values from -0.375 to 0.375
- head_bias: float32 [8, 14], P('member'), may hold values from -4 to 4
- prior_precision: float32 [8, 1024], P('member'), may hold values from 0.5 to 5
- labels: int32 [8192], P('dp'), may hold values from 0 to 13
- category_weight: int32 [14], replicated, may hold values from 1 to 9
Outputs:
- variance: float32 [8, 8192], P('member', 'dp')
- ensemble_probs: float32 [14, 8192], P(None, 'dp')
All inputs are finite; a program needn't handle non-finite values.
Results may differ from a plain program's by a relative error of at most 0.0025.
Values may be sent and summed in bfloat16 or wider, within the bound.
A program may use at most 128 MiB of HBM per device.

v0:
```python
import jax
import jax.numpy as jnp
from jax import lax
from jax.sharding import PartitionSpec as P


def body(hidden, projection, head_weight, head_bias, prior_precision, labels, category_weight):
    local_rows = hidden[0]
    weight_rows = projection[0]
    tok_rows = local_rows.shape[0]
    width = weight_rows.shape[1]
    categories = head_weight.shape[1]
    projected = jnp.dot(
        local_rows,
        lax.all_gather(weight_rows, "dp", axis=0, tiled=True),
        preferred_element_type=jnp.float32,
    )
    features = projected.astype(jnp.bfloat16)
    logits = (
        lax.dot_general(
            head_weight[0], features, (((1,), (1,)), ((), ())), preferred_element_type=jnp.float32
        )
        + head_bias[0][:, None]
    )
    onehot = labels[None, :] == jnp.arange(categories, dtype=jnp.int32)[:, None]
    row_weight = jnp.sum(
        jnp.where(onehot, category_weight.astype(jnp.float32)[:, None], jnp.float32(0.0)), axis=0
    )
    expo = jnp.exp(logits)
    probs = expo / jnp.sum(expo, axis=0, keepdims=True)
    curvature = row_weight * (1.0 - jnp.sum(probs * probs, axis=0))
    weighted = (features * jnp.sqrt(curvature)[:, None]).astype(jnp.bfloat16)
    gram_part = lax.dot_general(
        weighted, weighted, (((0,), (0,)), ((), ())), preferred_element_type=jnp.float32
    )
    rows_total = tok_rows * lax.axis_size("dp")
    prior = prior_precision[0]
    gram = lax.psum(gram_part, "dp")
    factor = jnp.linalg.cholesky(gram / rows_total + jnp.diag(prior))
    columns_f32 = features.T.astype(jnp.float32)
    solved = lax.linalg.triangular_solve(factor, columns_f32, left_side=True, lower=True)
    variance = 4.0 / width * jnp.sum(solved * solved, axis=0)
    scaled = logits / jnp.sqrt(1.0 + variance)[None, :]
    moder = jnp.exp(scaled)
    moder = moder / jnp.sum(moder, axis=0, keepdims=True)
    summed = lax.psum(moder, "member")
    ensemble = summed / lax.axis_size("member")
    return (variance[None, :], ensemble)


def solution(mesh):
    return jax.shard_map(
        body,
        mesh=mesh,
        in_specs=(
            P("member", "dp", None),
            P("member", "dp", None),
            P("member", None, None),
            P("member", None),
            P("member", None),
            P("dp"),
            P(),
        ),
        out_specs=(P("member", "dp"), P(None, "dp")),
        check_vma=False,
    )
```

profile of v0, /device:TPU:0, one launch (start us, length us, event | category | flops | bytes accessed | tf_op | source)
XLA Modules:
  0.0 645.7 jit_solution(16318952390802729198)
XLA Ops:
  9.4 76.3 %all-gather.3.cloned.1.call-done = bf16[1,4096,1024]{2,1,0:T(8,128)(2,1)} async-done(((bf16[1,256,1024]{2,1,0:T(8,128)(2,1)}), bf16[1,4096,1024]{2,1,0:T(8,128)(2,1)}) %all-gather.3.cloned.1.call-update) | async-done | bytes 8388624 | tf_op jit(solution)/shard_map/all_gather | solution.py:15
  85.6 10.5 %bitcast_convert_fusion = (f32[1024,512]{0,1:T(8,128)}, bf16[512,1024]{1,0:T(8,128)(2,1)S(1)}) fusion(bf16[1,4096,1024]{2,1,0:T(8,128)(2,1)} %all-gather.3.cloned.1.call-done, bf16[1,512,4096]{2,1,0:T(8,128)(2,1)} %param.7), kind=kOutput, calls=%fused_computation.177 | convolution fusion | flops 4296015872 | bytes 15728640 | tf_op jit(solution)/shard_map/dot_general | solution.py:13
  96.6 3.4 fusion.9
  100.1 148.5 %all-reduce.3.cloned.1.call-done = f32[1024,1024]{0,1:T(8,128)} async-done(((f32[1024,1024]{0,1:T(8,128)}), f32[1024,1024]{0,1:T(8,128)}) %all-reduce.3.cloned.1.call-update) | async-done | bytes 4194320 | tf_op jit(solution)/shard_map/psum | solution.py:38
  248.6 5.0 select_add_fusion
  253.6 5.5 copy.28
  259.2 4.5 fusion.2
  263.6 1.9 copy-done.2
  265.6 11.7 %cholesky.222 = f32[128,128]{1,0:T(8,128)S(1)} custom-call(f32[128,128]{1,0:T(8,128)S(1)} %cholesky.577), custom_call_target="Cholesky" | custom-call | tf_op jit(solution)/shard_map/jit(cholesky)/cholesky | solution.py:39
  277.4 9.8 %custom-call.62 = f32[1,128,128]{1,2,0:T(8,128)S(1)} custom-call(f32[1,128,128]{2,1,0:T(8,128)S(1)} %get-tuple-element.66), custom_call_target="InvertDiagBlocksLowerTriangular" | custom-call | tf_op jit(solution)/shard_map/jit(cholesky)/cholesky | solution.py:39
  290.5 11.7 %cholesky.243 = f32[128,128]{1,0:T(8,128)S(1)} custom-call(f32[128,128]{1,0:T(8,128)S(1)} %cholesky.581), custom_call_target="Cholesky" | custom-call | tf_op jit(solution)/shard_map/jit(cholesky)/cholesky | solution.py:39
  302.8 9.8 %custom-call.63 = f32[1,128,128]{1,2,0:T(8,128)S(1)} custom-call(f32[1,128,128]{2,1,0:T(8,128)S(1)} %get-tuple-element.64), custom_call_target="InvertDiagBlocksLowerTriangular" | custom-call | tf_op jit(solution)/shard_map/jit(cholesky)/cholesky | solution.py:39
  313.7 2.0 copy-done.1
  315.7 2.4 convolution_subtract_fusion.1
  318.1 11.7 %cholesky.466 = f32[128,128]{1,0:T(8,128)S(1)} custom-call(f32[128,128]{1,0:T(8,128)S(1)} %cholesky.586), custom_call_target="Cholesky" | custom-call | tf_op jit(solution)/shard_map/jit(cholesky)/cholesky | solution.py:39
  330.6 9.8 %custom-call.64 = f32[1,128,128]{1,2,0:T(8,128)S(1)} custom-call(f32[1,128,128]{2,1,0:T(8,128)S(1)} %get-tuple-element.62), custom_call_target="InvertDiagBlocksLowerTriangular" | custom-call | tf_op jit(solution)/shard_map/jit(cholesky)/cholesky | solution.py:39
  341.7 3.3 convolution_subtract_fusion.2
  345.0 11.7 %cholesky.485 = f32[128,128]{1,0:T(8,128)S(1)} custom-call(f32[128,128]{1,0:T(8,128)S(1)} %cholesky.591), custom_call_target="Cholesky" | custom-call | tf_op jit(solution)/shard_map/jit(cholesky)/cholesky | solution.py:39
  357.5 9.8 %custom-call.65 = f32[1,128,128]{1,2,0:T(8,128)S(1)} custom-call(f32[1,128,128]{2,1,0:T(8,128)S(1)} %get-tuple-element.60), custom_call_target="InvertDiagBlocksLowerTriangular" | custom-call | tf_op jit(solution)/shard_map/jit(cholesky)/cholesky | solution.py:39
  368.4 3.2 convolution_subtract_fusion.10
  371.6 12.1 %cholesky.504 = f32[128,128]{1,0:T(8,128)S(1)} custom-call(f32[128,128]{1,0:T(8,128)S(1)} %cholesky.596), custom_call_target="Cholesky" | custom-call | tf_op jit(solution)/shard_map/jit(cholesky)/cholesky | solution.py:39
  384.5 9.8 %custom-call.66 = f32[1,128,128]{1,2,0:T(8,128)S(1)} custom-call(f32[1,128,128]{2,1,0:T(8,128)S(1)} %get-tuple-element.58), custom_call_target="InvertDiagBlocksLowerTriangular" | custom-call | tf_op jit(solution)/shard_map/jit(cholesky)/cholesky | solution.py:39
  395.4 3.1 convolution_subtract_fusion.11
  398.5 11.7 %cholesky.524 = f32[128,128]{1,0:T(8,128)S(1)} custom-call(f32[128,128]{1,0:T(8,128)S(1)} %cholesky.601), custom_call_target="Cholesky" | custom-call | tf_op jit(solution)/shard_map/jit(cholesky)/cholesky | solution.py:39
  411.0 9.8 %custom-call.67 = f32[1,128,128]{1,2,0:T(8,128)S(1)} custom-call(f32[1,128,128]{2,1,0:T(8,128)S(1)} %get-tuple-element.56), custom_call_target="InvertDiagBlocksLowerTriangular" | custom-call | tf_op jit(solution)/shard_map/jit(cholesky)/cholesky | solution.py:39
  421.8 2.8 convolution_subtract_fusion.12
  424.6 11.7 %cholesky.544 = f32[128,128]{1,0:T(8,128)S(1)} custom-call(f32[128,128]{1,0:T(8,128)S(1)} %cholesky.606), custom_call_target="Cholesky" | custom-call | tf_op jit(solution)/shard_map/jit(cholesky)/cholesky | solution.py:39
  437.1 9.8 %custom-call.68 = f32[1,128,128]{1,2,0:T(8,128)S(1)} custom-call(f32[1,128,128]{2,1,0:T(8,128)S(1)} %get-tuple-element.54), custom_call_target="InvertDiagBlocksLowerTriangular" | custom-call | tf_op jit(solution)/shard_map/jit(cholesky)/cholesky | solution.py:39
  447.9 2.1 convolution_subtract_fusion.13
  450.0 11.7 %cholesky.562 = f32[128,128]{1,0:T(8,128)S(1)} custom-call(f32[128,128]{1,0:T(8,128)S(1)} %convolution_subtract_fusion.13), custom_call_target="Cholesky" | custom-call | tf_op jit(solution)/shard_map/jit(cholesky)/cholesky | solution.py:39
  472.0 4.8 select_select_fusion
  476.9 23.9 %while.1 = (s32[]{:T(128)}, f32[1024,1024]{0,1:T(8,128)}, s32[8,2]{0,1:T(2,128)S(1)}, f32[8,128,128]{2,1,0:T(8,128)S(1)}, s32[]{:T(128)}) while((s32[]{:T(128)}, f32[1024,1024]{0,1:T(8,128)}, s32[8,2]{0,1:T(2,128)S(1)}, f32[8,128,128]{2,1,0:T(8,128)S(1)}, s32[]{:T(128)}) %tuple.58), condition=%wide.while_cond, body=%wide.while_body.sunk | while | flops 2 | bytes 393329 | solution.py:41
  477.5 2.3 dynamic-slice.7
  480.5 2.3 dynamic-slice.7
  483.5 2.3 dynamic-slice.7
  486.4 2.3 dynamic-slice.7
  489.4 2.3 dynamic-slice.7
  492.4 2.3 dynamic-slice.7
  495.4 2.3 dynamic-slice.7
  498.4 2.2 dynamic-slice.7
  500.8 78.8 %custom-call.69 = f32[8,128,128]{1,2,0:T(8,128)S(1)} custom-call(f32[8,128,128]{2,1,0:T(8,128)S(1)} %get-tuple-element.9), custom_call_target="InvertDiagBlocksLowerTriangular" | custom-call | tf_op jit(solution)/shard_map/triangular_solve | solution.py:41
  582.2 2.0 convolution_subtract_fusion.5
  584.7 2.5 convolution_subtract_fusion.8
  587.7 2.8 convolution_subtract_fusion.9
  590.9 3.2 convolution_subtract_fusion.4
  594.6 3.6 convolution_subtract_fusion.7
  598.7 4.3 convolution_subtract_fusion.3
  604.3 33.5 %psum.15 = f32[14,512]{1,0:T(8,128)S(1)} all-reduce(f32[14,512]{1,0:T(8,128)S(1)} %divide_bitcast_fusion), channel_id=1, replica_groups=mesh['member'=8,'dp'=16] {'member'}, use_global_device_ids=true, to_apply=%region_22.23 | all-reduce | flops 7168 | bytes 57344 | tf_op jit(solution)/shard_map/psum | solution.py:46
  (116 shorter events, 34.8 us)
Async XLA Ops:
  7.2 89.0 %copy-start = (bf16[1,14,1024]{2,1,0:T(8,128)(2,1)S(1)}, bf16[1,14,1024]{2,1,0:T(8,128)(2,1)}, u32[]{:S(2)}) copy-start(bf16[1,14,1024]{2,1,0:T(8,128)(2,1)} %param.9) | copy-start | bytes 86020
  7.2 78.5 %all-gather.3.cloned.1.call-start = ((), (), s32[]{:S(2)}) async-start(), calls=%async_computation.1 | async-start | bytes 8912896 | tf_op jit(solution)/shard_map/all_gather | solution.py:15
  7.9 240.7 %all-reduce.3.cloned.1.call-start = ((), (), s32[]{:S(2)}) async-start(), calls=%async_computation | async-start | bytes 8388608 | tf_op jit(solution)/shard_map/psum | solution.py:38
  9.4 86.8 %copy-start.5 = (f32[1,14]{1,0:T(1,128)S(1)}, f32[1,14]{1,0:T(1,128)}, u32[]{:S(2)}) copy-start(f32[1,14]{1,0:T(1,128)} %param.10) | copy-start | bytes 172
  100.0 148.6 %copy-start.4 = (f32[1,1024]{1,0:T(1,128)S(1)}, f32[1,1024]{1,0:T(1,128)}, u32[]{:S(2)}) copy-start(f32[1,1024]{1,0:T(1,128)} %param.11) | copy-start | bytes 12292
  263.6 1.9 copy-start.2
  313.7 2.0 copy-start.1
  580.0 7.7 %copy-start.3 = (f32[1024,512]{0,1:T(8,128)S(1)}, f32[1024,512]{0,1:T(8,128)}, u32[]{:S(2)}) copy-start(f32[1024,512]{0,1:T(8,128)} %get-tuple-element.72) | copy-start | bytes 6291460
Sparse Core Ops, SparseCore 0:
  10.5 75.1 all-gather.2
  100.2 148.3 all-reduce.2
where the time goes:
time: 652 us; the launch traced here: 646 us
  other arithmetic  264 us (40%)
  waiting for transfers between devices  225 us (35%)
  matrix products  63.9 us (10%)
  local copies, waits for them, and re-layouts  38.8 us (6%)
  blocking collectives  33.5 us (5%)
  between operations  19.9 us (3%)
    another operation x30, other arithmetic, body(): factor = jnp.linalg.cholesky(gram / rows_total + jnp.diag(prior))  168 us
    psum x1, waiting for transfers between devices, body(): gram = lax.psum(gram_part, 'dp')  149 us
    another operation x3, other arithmetic, body(): lax.linalg.triangular_solve(factor, columns_f32, left_side=True, lower=True)  83.6 us
    all_gather x1, waiting for transfers between devices, body(): lax.all_gather(weight_rows, 'dp', axis=0, tiled=True)  76.3 us
    psum x1, blocking collectives, body(): summed = lax.psum(moder, 'member')  33.5 us
    another operation x14, matrix products, body(): factor = jnp.linalg.cholesky(gram / rows_total + jnp.diag(prior))  25.9 us
    another operation x15, matrix products, body(): lax.linalg.triangular_solve(factor, columns_f32, left_side=True, lower=True)  23.7 us
    another operation x40, local copies, waits for them, and re-layouts  23.6 us
  transfers between devices with their start and end apart: 2, of which 2 were waited for; matrix products, arithmetic and copies ran while one was open for 0% of the time, Pallas kernels for 0%

commit v1 on v0

v1 whole, which is shorter than its diff:
```python
import jax, jax.numpy as jnp
from jax import lax
from jax.experimental import pallas as pl
from jax.experimental.pallas import tpu as pltpu
from jax.sharding import PartitionSpec as P

N = 1024
ROWS = 8192
B = 128
NB = N // B
R_ = 512
W = N + R_
f32 = jnp.float32
bf16 = jnp.bfloat16


def split3(x):
    hi = x.astype(bf16)
    lo = (x - hi.astype(f32)).astype(bf16)
    return hi, lo


def diag_inverse(S):
    G = 8
    n = B // G
    R = list(S)
    lane = lax.broadcasted_iota(jnp.int32, (G, B), 1)
    sub = lax.broadcasted_iota(jnp.int32, (G, B), 0)
    Q = [jnp.where(lane == sub + G * i, f32(1), f32(0)) for i in range(n)]
    out = [None] * n
    for b in range(n):
        c = [[jnp.broadcast_to(R[i][:, G * b + k:G * b + k + 1], (G, B)) for k in range(G)] for i in range(b, n)]
        cb = c[0]
        rb, qb = R[b], Q[b]
        dv = jnp.ones((G, B), f32)
        inv, rj, qj, cs = [], [], [], []
        for j in range(G):
            p = jnp.broadcast_to(cb[j][j:j + 1, :], (G, B))
            iv = 1.0 / p
            dv = jnp.where(sub == j, p, dv)
            m = jnp.where(sub > j, cb[j] * iv, f32(0))
            row = [None] * G
            for k in range(j + 1, G):
                row[k] = jnp.broadcast_to(cb[k][j:j + 1, :], (G, B))
                cb[k] = cb[k] - m * row[k]
            r = jnp.broadcast_to(rb[j:j + 1, :], (G, B))
            q = jnp.broadcast_to(qb[j:j + 1, :], (G, B))
            if j < G - 1:
                rb = rb - m * r
                qb = qb - m * q
            inv.append(iv); rj.append(r); qj.append(q); cs.append(row)
        out[b] = qb * lax.rsqrt(dv)
        for i in range(b + 1, n):
            ci = c[i - b]
            ri, qi = R[i], Q[i]
            for j in range(G):
                m = ci[j] * inv[j]
                for k in range(j + 1, G):
                    ci[k] = ci[k] - m * cs[j][k]
                ri = ri - m * rj[j]
                qi = qi - m * qj[j]
            R[i], Q[i] = ri, qi
    return out


def chol_kernel(a_ref, prior_ref, ft_ref, var_ref, g_ref, linv_ref, ul_ref, ur_ref):
    eye_r = lax.broadcasted_iota(jnp.int32, (B, N), 0)
    eye_c = lax.broadcasted_iota(jnp.int32, (B, N), 1)
    for i in range(NB):
        rows = pl.ds(B * i, B)
        g_ref[rows, :N] = a_ref[rows, :] * f32(1.0 / ROWS) + jnp.where(eye_c == eye_r + B * i, prior_ref[...], f32(0))
        g_ref[rows, N:] = ft_ref[rows, :].astype(f32)
    var_ref[...] = jnp.zeros_like(var_ref)

    @pl.loop(0, NB)
    def _(k):
        k0 = pl.multiple_of(k * B, B)
        S = [g_ref[pl.ds(k0 + 8 * i, 8), pl.ds(k0, B)] for i in range(16)]
        out = diag_inverse(S)
        for i in range(16):
            linv_ref[pl.ds(8 * i, 8), :] = out[i]
        li = linv_ref[...]
        lh, ll = split3(li)
        lcat = jnp.concatenate([lh, ll, lh], axis=1)
        CW = 512
        for c in range(W // CW):
            gh, gl = split3(g_ref[pl.ds(k0, B), CW * c:CW * (c + 1)])
            u = jnp.dot(lcat, jnp.concatenate([gh, gh, gl], axis=0), preferred_element_type=f32)
            uh, ul = split3(u)
            ur_ref[0:B, CW * c:CW * (c + 1)] = uh
            ur_ref[B:2 * B, CW * c:CW * (c + 1)] = uh
            ur_ref[2 * B:, CW * c:CW * (c + 1)] = ul
            if c < N // CW:
                for t in range(CW // B):
                    ut = u[:, B * t:B * (t + 1)].T
                    th, tl = split3(ut)
                    r0 = CW * c + B * t
                    ul_ref[r0:r0 + B, 0:B] = th
                    ul_ref[r0:r0 + B, B:2 * B] = tl
                    ul_ref[r0:r0 + B, 2 * B:] = th
            else:
                var_ref[...] += jnp.sum(u * u, axis=0, keepdims=True)

        @pl.loop(k + 1, NB)
        def _(i):
            i0 = pl.multiple_of(i * B, B)
            lhs = ul_ref[pl.ds(i0, B), :]
            for c in range(W // CW):
                d = jnp.dot(lhs, ur_ref[:, CW * c:CW * (c + 1)], preferred_element_type=f32)
                g_ref[pl.ds(i0, B), CW * c:CW * (c + 1)] -= d
    var_ref[...] = var_ref[...] * (4.0 / N)


def chol_var(a, prior, ft):
    return pl.pallas_call(
        chol_kernel,
        out_shape=jax.ShapeDtypeStruct((1, R_), f32),
        in_specs=[pl.BlockSpec(memory_space=pltpu.VMEM)] * 3,
        out_specs=pl.BlockSpec(memory_space=pltpu.VMEM),
        scratch_shapes=[
            pltpu.VMEM((N, W), f32),
            pltpu.VMEM((B, B), f32),
            pltpu.VMEM((N, 3 * B), bf16),
            pltpu.VMEM((3 * B, W), bf16),
        ],
        compiler_params=pltpu.CompilerParams(vmem_limit_bytes=48 * 1024 * 1024),
    )(a, prior, ft)


def body(hidden, projection, head_weight, head_bias, prior_precision, labels, category_weight):
    local_rows = hidden[0]
    weight_rows = projection[0]
    categories = head_weight.shape[1]
    projected = jnp.dot(
        local_rows,
        lax.all_gather(weight_rows, "dp", axis=0, tiled=True),
        preferred_element_type=f32,
    )
    features = projected.astype(bf16)
    logits = (
        lax.dot_general(head_weight[0], features, (((1,), (1,)), ((), ())), preferred_element_type=f32)
        + head_bias[0][:, None]
    )
    onehot = labels[None, :] == jnp.arange(categories, dtype=jnp.int32)[:, None]
    row_weight = jnp.sum(jnp.where(onehot, category_weight.astype(f32)[:, None], f32(0.0)), axis=0)
    expo = jnp.exp(logits)
    probs = expo / jnp.sum(expo, axis=0, keepdims=True)
    curvature = row_weight * (1.0 - jnp.sum(probs * probs, axis=0))
    weighted = (features * jnp.sqrt(curvature)[:, None]).astype(bf16)
    gram_part = lax.dot_general(weighted, weighted, (((0,), (0,)), ((), ())), preferred_element_type=f32)
    gram = lax.psum(gram_part, "dp")
    variance = chol_var(gram, prior_precision, features.T)[0]
    scaled = logits / jnp.sqrt(1.0 + variance)[None, :]
    moder = jnp.exp(scaled)
    moder = moder / jnp.sum(moder, axis=0, keepdims=True)
    summed = lax.psum(moder, "member")
    ensemble = summed / lax.axis_size("member")
    return (variance[None, :], ensemble)


def solution(mesh):
    return jax.shard_map(
        body,
        mesh=mesh,
        in_specs=(
            P("member", "dp", None),
            P("member", "dp", None),
            P("member", None, None),
            P("member", None),
            P("member", None),
            P("dp"),
            P(),
        ),
        out_specs=(P("member", "dp"), P(None, "dp")),
        check_vma=False,
    )
```

time: 652 us -> 338 us (0.52)
  other arithmetic: 264 us -> 2.84 us
  matrix products: 63.9 us -> 12.7 us
  Pallas kernels: 0 us -> 46.9 us
  local copies, waits for them, and re-layouts: 38.8 us -> 2.2 us
    another operation x33 -> x0, other arithmetic: 251 us -> none  [the longest x30 168 us: body(): factor = jnp.linalg.cholesky(gram / rows_total + jnp.diag(prior))]
    another operation x29 -> x0, matrix products: 49.6 us -> none  [the longest x14 25.9 us: body(): factor = jnp.linalg.cholesky(gram / rows_total + jnp.diag(prior))]
    pallas_call x0 -> x1, Pallas kernels: none -> 46.9 us  [chol_var(): pl.pallas_call(chol_kernel, out_shape=jax.ShapeDtypeStruct((1, R_), f32),...]
    another operation x66 -> x0, local copies, waits for them, and re-layouts: 29.4 us -> none
where the time goes in v1:
time: 338 us
  waiting for transfers between devices  225 us (67%)
  Pallas kernels  46.9 us (14%)
  blocking collectives  33.5 us (10%)
  between operations  14.1 us (4%)
  matrix products  12.7 us (4%)
    psum x1, waiting for transfers between devices, body(): gram = lax.psum(gram_part, 'dp')  148 us
    all_gather x1, waiting for transfers between devices, body(): lax.all_gather(weight_rows, 'dp', axis=0, tiled=True)  76.3 us
    pallas_call x1, Pallas kernels, chol_var(): pl.pallas_call(chol_kernel, out_shape=jax.ShapeDtypeStruct((1, R_), f32),...  46.9 us
    psum x1, blocking collectives, body(): summed = lax.psum(moder, 'member')  33.5 us
    dot_general x1, matrix products, body(): jnp.dot(local_rows, lax.all_gather(weight_rows, 'dp', axis=0, tiled=True)...  9.19 us
  transfers between devices with their start and end apart: 2, of which 2 were waited for; matrix products, arithmetic and copies ran while one was open for 0% of the time, Pallas kernels for 0%

profile of v1, /device:TPU:0, one launch (start us, length us, event | category | flops | bytes accessed | tf_op | source)
XLA Modules:
  0.0 337.8 jit_solution(12062176300711893602)
XLA Ops:
  7.2 0.0 copy-start
  7.2 0.0 all-gather.3.cloned.1.call-start
  7.2 0.7 all-gather.3.cloned.1.call-update
  7.9 0.0 all-reduce.2.cloned.1.call-start
  8.0 0.7 convert_element_type.18
  8.6 0.8 select_reduce_fusion
  9.4 0.0 copy-start.3
  9.4 76.3 %all-gather.3.cloned.1.call-done = bf16[1,4096,1024]{2,1,0:T(8,128)(2,1)} async-done(((bf16[1,256,1024]{2,1,0:T(8,128)(2,1)}), bf16[1,4096,1024]{2,1,0:T(8,128)(2,1)}) %all-gather.3.cloned.1.call-update) | async-done | bytes 8388624 | tf_op jit(solution)/shard_map/all_gather | solution.py:136
  85.6 9.2 %fusion.3 = bf16[512,1024]{0,1:T(8,128)(2,1)S(1)} fusion(bf16[1,4096,1024]{2,1,0:T(8,128)(2,1)} %all-gather.3.cloned.1.call-done, bf16[1,512,4096]{2,1,0:T(8,128)(2,1)} %param.7), kind=kOutput, calls=%fused_computation.4 | convolution fusion | flops 4295491584 | bytes 13631488 | tf_op jit(solution)/shard_map/dot_general | solution.py:134
  94.8 0.0 copy-done
  94.8 0.0 copy-done.3
  94.9 0.3 exponential_reduce_fusion
  95.2 3.3 fusion.8
  98.5 0.0 copy-start.2
  98.5 0.0 all-reduce.2.cloned.1.call-update
  98.5 148.5 %all-reduce.2.cloned.1.call-done.a_ref = f32[1024,1024]{1,0:T(8,128)} async-done(((f32[1024,1024]{1,0:T(8,128)}), f32[1024,1024]{1,0:T(8,128)}) %all-reduce.2.cloned.1.call-update) | async-done | bytes 4194320 | tf_op jit(solution)/shard_map/psum | solution.py:151
  246.9 0.0 copy-done.2
  246.9 0.0 copy-start.1
  246.9 2.2 copy-done.1
  249.1 46.9 %shard_map.86 = f32[1,512]{1,0:T(1,128)} custom-call(f32[1024,1024]{1,0:T(8,128)S(1)} %copy-done.1, f32[1,1024]{1,0:T(1,128)S(1)} %copy-done.2, bf16[1024,512]{1,0:T(8,128)(2,1)S(1)} %bitcast.21), custom_call_target="tpu_custom_call" | custom-call | tf_op jit(solution)/shard_map/pallas_call | solution.py:115
  296.1 0.7 add_sqrt_fusion
  296.8 33.5 %psum.15 = f32[14,512]{1,0:T(8,128)S(1)} all-reduce(f32[14,512]{1,0:T(8,128)S(1)} %divide_bitcast_fusion), channel_id=1, replica_groups=mesh['member'=8,'dp'=16] {'member'}, use_global_device_ids=true, to_apply=%region_5.6 | all-reduce | flops 7168 | bytes 57344 | tf_op jit(solution)/shard_map/psum | solution.py:156
  330.3 0.6 broadcast_multiply_fusion
  (4 shorter events, 0.1 us)
Async XLA Ops:
  7.2 87.7 %copy-start = (bf16[1,14,1024]{2,1,0:T(8,128)(2,1)S(1)}, bf16[1,14,1024]{2,1,0:T(8,128)(2,1)}, u32[]{:S(2)}) copy-start(bf16[1,14,1024]{2,1,0:T(8,128)(2,1)} %param.9) | copy-start | bytes 86020
  7.2 78.5 %all-gather.3.cloned.1.call-start = ((), (), s32[]{:S(2)}) async-start(), calls=%async_computation.1 | async-start | bytes 8912896 | tf_op jit(solution)/shard_map/all_gather | solution.py:136
  7.9 239.0 %all-reduce.2.cloned.1.call-start = ((), (), s32[]{:S(2)}) async-start(), calls=%async_computation | async-start | bytes 8388608 | tf_op jit(solution)/shard_map/psum | solution.py:151
  9.4 85.5 %copy-start.3 = (f32[1,14]{1,0:T(1,128)S(1)}, f32[1,14]{1,0:T(1,128)}, u32[]{:S(2)}) copy-start(f32[1,14]{1,0:T(1,128)} %param.10) | copy-start | bytes 172
  98.5 148.5 %copy-start.2 = (f32[1,1024]{1,0:T(1,128)S(1)}, f32[1,1024]{1,0:T(1,128)}, u32[]{:S(2)}) copy-start(f32[1,1024]{1,0:T(1,128)} %prior_ref.1) | copy-start | bytes 12292
  246.9 2.2 copy-start.1
Sparse Core Ops, SparseCore 0:
  10.5 75.1 all-gather.2
  98.6 148.2 all-reduce.1

commit v2 on v1

--- a/solution.py
+++ b/solution.py
@@ -5,6 +5,7 @@
 from jax.sharding import PartitionSpec as P
 
 N = 1024
+P_SIZE = 1024
 ROWS = 8192
 B = 128
 NB = N // B
@@ -127,29 +128,178 @@
     )(a, prior, ft)
 
 
-def body(hidden, projection, head_weight, head_bias, prior_precision, labels, category_weight):
-    local_rows = hidden[0]
-    weight_rows = projection[0]
-    categories = head_weight.shape[1]
-    projected = jnp.dot(
-        local_rows,
-        lax.all_gather(weight_rows, "dp", axis=0, tiled=True),
-        preferred_element_type=f32,
-    )
-    features = projected.astype(bf16)
-    logits = (
-        lax.dot_general(head_weight[0], features, (((1,), (1,)), ((), ())), preferred_element_type=f32)
-        + head_bias[0][:, None]
-    )
-    onehot = labels[None, :] == jnp.arange(categories, dtype=jnp.int32)[:, None]
-    row_weight = jnp.sum(jnp.where(onehot, category_weight.astype(f32)[:, None], f32(0.0)), axis=0)
+MESH = pl.DeviceIdType.MESH
+C = 14
+KB = 256
+
+
+def gather_kernel(hid_ref, proj_ref, hw_ref, hb_ref, lab_ref, cw_ref, ft_ref, gram_ref, log_ref,
+                  h_ref, buf_ref, acc_ref, wt_ref, loc_sem, send_sem, recv_sem):
+    m = lax.axis_index("member")
+    d = lax.axis_index("dp")
+    c = lax.rem(d, 2)
+    x = lax.rem(d // 2, 4)
+    yh = d // 8
+
+    def dp(dy, dx, t):
+        yy = yh if dy == 0 else 1 - yh
+        cc = c if t == 0 else 1 - c
+        return (yy * 4 + lax.rem(x + dx, 4)) * 2 + cc
+
+    to_r, to_l, to_y, to_m = dp(0, 1, 0), dp(0, 3, 0), dp(1, 0, 0), dp(0, 0, 1)
+    me = d
+    own_copy = pltpu.make_async_copy(proj_ref, buf_ref.at[me], loc_sem.at[0])
+    own_copy.start()
+    hid_copy = pltpu.make_async_copy(hid_ref, h_ref, loc_sem.at[1])
+    hid_copy.start()
+    bar = pltpu.get_barrier_semaphore()
+    for t in (to_r, to_l, to_y, to_m):
+        pl.semaphore_signal(bar, inc=1, device_id=(m, t), device_id_type=MESH)
+    pl.semaphore_wait(bar, 4)
+    own_copy.wait()
+    sends = []
+
+    def half(s, h):
+        return buf_ref.at[s, pl.ds(h * (KB // 2), KB // 2), :]
+
+    def copy(s, h, to, i):
+        return pltpu.make_async_remote_copy(
+            src_ref=half(s, h), dst_ref=half(s, h), send_sem=send_sem.at[i], recv_sem=recv_sem.at[s, h],
+            device_id=(m, to), device_id_type=MESH)
+
+    def send(to, s, h):
+        cp = copy(s, h, to, len(sends))
+        cp.start()
+        sends.append(cp)
+
+    def wait(s, h):
+        copy(s, h, to_m, 0).wait_recv()
+
+    def mm(s, first=False):
+        k0 = pl.multiple_of(s * KB, KB)
+
+        @pl.loop(0, P_SIZE // 256)
+        def _(n):
+            n0 = pl.multiple_of(n * 256, 256)
+            r = jnp.dot(h_ref[:, pl.ds(k0, KB)], buf_ref[s, :, pl.ds(n0, 256)], preferred_element_type=f32)
+            if first:
+                acc_ref[:, pl.ds(n0, 256)] = r
+            else:
+                acc_ref[:, pl.ds(n0, 256)] += r
+
+    send(to_r, me, 0)
+    send(to_l, me, 1)
+    send(to_y, me, 0)
+    send(to_y, me, 1)
+    send(to_r, me, 1)
+    send(to_l, me, 0)
+    send(to_m, me, 0)
+    send(to_m, me, 1)
+    hid_copy.wait()
+    mm(me, True)
+    mate = dp(0, 0, 1)
+    wait(mate, 0)
+    wait(mate, 1)
+    mm(mate)
+    left, right, anti, part = dp(0, 3, 0), dp(0, 1, 0), dp(0, 2, 0), dp(1, 0, 0)
+    wait(left, 0)
+    send(to_r, left, 0)
+    wait(right, 1)
+    send(to_l, right, 1)
+    send(to_m, left, 0)
+    send(to_m, right, 1)
+    for h in (0, 1):
+        wait(part, h)
+        send(to_r, part, h)
+        send(to_l, part, h)
+        send(to_m, part, h)
+    wait(left, 1)
+    send(to_m, left, 1)
+    wait(right, 0)
+    send(to_m, right, 0)
+    mm(left)
+    mm(right)
+    for h in (0, 1):
+        wait(anti, h)
+        send(to_y, anti, h)
+        send(to_m, anti, h)
+    mm(part)
+    for s in (dp(0, 3, 1), dp(0, 1, 1), dp(1, 0, 1)):
+        wait(s, 0)
+        wait(s, 1)
+        mm(s)
+    mm(anti)
+    s = dp(0, 2, 1)
+    wait(s, 0)
+    wait(s, 1)
+    mm(s)
+    pl_, pr, pa = dp(1, 3, 0), dp(1, 1, 0), dp(1, 2, 0)
+    for h in (0, 1):
+        wait(pl_, h)
+        send(to_m, pl_, h)
+        wait(pr, h)
+        send(to_m, pr, h)
+    mm(pl_)
+    mm(pr)
+    for h in (0, 1):
+        wait(pa, h)
+        send(to_m, pa, h)
+    mm(pa)
+    for s in (dp(1, 3, 1), dp(1, 1, 1), dp(1, 2, 1)):
+        wait(s, 0)
+        wait(s, 1)
+        mm(s)
+
+    for j in range(NB):
+        ft_ref[B * j:B * (j + 1), :] = acc_ref[:, B * j:B * (j + 1)].T.astype(bf16)
+    logits = jnp.dot(hw_ref[...], ft_ref[...], preferred_element_type=f32) + hb_ref[...]
+    log_ref[...] = logits
+    cat = lax.broadcasted_iota(jnp.int32, (C, R_), 0)
+    row_weight = jnp.sum(jnp.where(cat == lab_ref[...], cw_ref[...].astype(f32), f32(0)), axis=0, keepdims=True)
     expo = jnp.exp(logits)
     probs = expo / jnp.sum(expo, axis=0, keepdims=True)
-    curvature = row_weight * (1.0 - jnp.sum(probs * probs, axis=0))
-    weighted = (features * jnp.sqrt(curvature)[:, None]).astype(bf16)
-    gram_part = lax.dot_general(weighted, weighted, (((0,), (0,)), ((), ())), preferred_element_type=f32)
+    curv = row_weight * (1.0 - jnp.sum(probs * probs, axis=0, keepdims=True))
+    root = jnp.sqrt(curv)
+    for j in range(NB):
+        wt_ref[B * j:B * (j + 1), :] = (ft_ref[B * j:B * (j + 1), :].astype(f32) * root).astype(bf16)
+    for i in range(4):
+        gram_ref[256 * i:256 * (i + 1), 256 * i:] = lax.dot_general(
+            wt_ref[256 * i:256 * (i + 1), :], wt_ref[256 * i:, :], (((1,), (1,)), ((), ())), preferred_element_type=f32)
+    for cp in sends:
+        cp.wait_send()
+
+
+def gather_features(hidden, proj, hw, hb, labels, cw):
+    vm = pl.BlockSpec(memory_space=pltpu.VMEM)
+    any_ = pl.BlockSpec(memory_space=pl.ANY)
+    return pl.pallas_call(
+        gather_kernel,
+        out_shape=(
+            jax.ShapeDtypeStruct((N, R_), bf16),
+            jax.ShapeDtypeStruct((N, N), f32),
+            jax.ShapeDtypeStruct((C, R_), f32),
+        ),
+        in_specs=[any_, any_, vm, vm, vm, vm],
+        out_specs=(vm, vm, vm),
+        scratch_shapes=[
+            pltpu.VMEM((R_, 4096), bf16),
+            pltpu.VMEM((16, KB, P_SIZE), bf16),
+            pltpu.VMEM((R_, P_SIZE), f32),
+            pltpu.VMEM((N, R_), bf16),
+            pltpu.SemaphoreType.DMA((2,)),
+            pltpu.SemaphoreType.DMA((30,)),
+            pltpu.SemaphoreType.DMA((16, 2)),
+        ],
+        compiler_params=pltpu.CompilerParams(
+            collective_id=0, has_side_effects=True, vmem_limit_bytes=48 * 1024 * 1024),
+    )(hidden, proj, hw, hb, labels, cw)
+
+
+def body(hidden, projection, head_weight, head_bias, prior_precision, labels, category_weight):
+    ft, gram_part, logits = gather_features(
+        hidden[0], projection[0], head_weight[0], head_bias[0][:, None], labels[None, :], category_weight[:, None])
     gram = lax.psum(gram_part, "dp")
-    variance = chol_var(gram, prior_precision, features.T)[0]
+    variance = chol_var(gram, prior_precision, ft)[0]
     scaled = logits / jnp.sqrt(1.0 + variance)[None, :]
     moder = jnp.exp(scaled)
     moder = moder / jnp.sum(moder, axis=0, keepdims=True)

time: 338 us -> 297 us (0.88)
  waiting for transfers between devices: 225 us -> 150 us
  Pallas kernels: 46.9 us -> 89.1 us
  matrix products: 12.7 us -> 0 us
  local copies, waits for them, and re-layouts: 2.2 us -> 8.11 us
    all_gather x1 -> x0, waiting for transfers between devices: 76.3 us -> none  [body(): lax.all_gather(weight_rows, 'dp', axis=0, tiled=True)]
    pallas_call x0 -> x1, Pallas kernels: none -> 42.2 us  [gather_features(): pl.pallas_call(gather_kernel, out_shape=(jax.ShapeDtypeStruct((N, R_), bf...]
    dot_general x3 -> x0, matrix products: 12.7 us -> none  [the longest x1 9.19 us: body(): jnp.dot(local_rows, lax.all_gather(weight_rows, 'dp', axis=0, tiled=True)...]
    unnamed x8 -> x12, local copies, waits for them, and re-layouts: 2.2 us -> 6.62 us
  transfers between devices with their start and end apart: 2 -> 1, of which waited for: 2 -> 1; matrix products, arithmetic and copies ran while one was open for 0% -> 0% of each run, Pallas kernels for 0% -> 0%
where the time goes in v2:
time: 297 us; the launch traced here: 296 us
  waiting for transfers between devices  150 us (51%)
  Pallas kernels  89.1 us (30%)
  blocking collectives  33.6 us (11%)
  between operations  14.1 us (5%)
  local copies, waits for them, and re-layouts  8.11 us (3%)
    psum x1, waiting for transfers between devices, body(): gram = lax.psum(gram_part, 'dp')  150 us
    pallas_call x1, Pallas kernels, chol_var(): pl.pallas_call(chol_kernel, out_shape=jax.ShapeDtypeStruct((1, R_), f32),...  46.9 us
    pallas_call x1, Pallas kernels, gather_features(): pl.pallas_call(gather_kernel, out_shape=(jax.ShapeDtypeStruct((N, R_), bf...  42.2 us
    psum x1, blocking collectives, body(): summed = lax.psum(moder, 'member')  33.6 us
    unnamed x12, local copies, waits for them, and re-layouts  6.62 us
  transfers between devices with their start and end apart: 1, of which 1 were waited for; matrix products, arithmetic and copies ran while one was open for 0% of the time, Pallas kernels for 0%

profile of v2, /device:TPU:0, one launch (start us, length us, event | category | flops | bytes accessed | tf_op | source)
XLA Modules:
  0.0 296.2 jit_solution(15609088788564493024)
XLA Ops:
  7.2 0.0 all-reduce.2.cloned.1.call-start
  7.2 0.7 copy.9.hb_ref
  8.0 0.7 copy.10.cw_ref
  8.7 0.0 copy-start.2
  8.7 1.0 copy-done.2
  9.7 0.0 copy-start.3
  9.7 0.8 copy-done.3
  10.5 0.0 copy-start.5
  10.5 0.7 copy-done.5
  11.2 0.0 copy-start.4
  11.2 42.2 %shard_map.86 = (bf16[1024,512]{1,0:T(8,128)(2,1)S(1)}, f32[1024,1024]{1,0:T(8,128)S(1)}, f32[14,512]{1,0:T(8,128)S(1)}) custom-call(bf16[512,4096]{1,0:T(8,128)(2,1)} %bitcast.10, bf16[256,1024]{1,0:T(8,128)(2,1)S(1)} %bitcast.7, bf16[14,1024]{1,0:T(8,128)(2,1)S(1)} %bitcast.8, f32[14,1]{1,0:T(8,128)S(1)} %copy.9.hb_ref, s32[1,512]{1,0:T(1,128)S(1)} %bitcast.9, ...), custom_call_target="tpu_custom_call" | custom-call | tf_op jit(solution)/shard_map/pallas_call | solution.py:275
  53.4 0.0 copy-start
  53.4 2.0 copy-done
  55.4 0.0 all-reduce.2.cloned.1.call-update
  55.4 149.9 %all-reduce.2.cloned.1.call-done.a_ref = f32[1024,1024]{1,0:T(8,128)} async-done(((f32[1024,1024]{1,0:T(8,128)}), f32[1024,1024]{1,0:T(8,128)}) %all-reduce.2.cloned.1.call-update) | async-done | bytes 4194320 | tf_op jit(solution)/shard_map/psum | solution.py:301
  205.3 0.0 copy-done.4
  205.3 0.0 copy-start.1
  205.3 2.2 copy-done.1
  207.5 46.9 %shard_map.87 = f32[1,512]{1,0:T(1,128)} custom-call(f32[1024,1024]{1,0:T(8,128)S(1)} %copy-done.1, f32[1,1024]{1,0:T(1,128)S(1)} %copy-done.4, bf16[1024,512]{1,0:T(8,128)(2,1)S(1)} %get-tuple-element.6.ft_ref), custom_call_target="tpu_custom_call" | custom-call | tf_op jit(solution)/shard_map/pallas_call | solution.py:116
  254.4 0.7 add_sqrt_fusion
  255.1 33.6 %psum.15 = f32[14,512]{1,0:T(8,128)S(1)} all-reduce(f32[14,512]{1,0:T(8,128)S(1)} %broadcast_divide_fusion), channel_id=1, replica_groups=mesh['member'=8,'dp'=16] {'member'}, use_global_device_ids=true, to_apply=%region_2.0 | all-reduce | flops 7168 | bytes 57344 | tf_op jit(solution)/shard_map/psum | solution.py:306
  288.7 0.6 broadcast_multiply_fusion
  (2 shorter events, 0.1 us)
Async XLA Ops:
  7.2 198.1 %all-reduce.2.cloned.1.call-start = ((), (), s32[]{:S(2)}) async-start(), calls=%async_computation | async-start | bytes 8388608 | tf_op jit(solution)/shard_map/psum | solution.py:301
  8.7 1.0 copy-start.2
  9.7 0.8 copy-start.3
  10.5 0.7 copy-start.5
  11.2 194.1 %copy-start.4 = (f32[1,1024]{1,0:T(1,128)S(1)}, f32[1,1024]{1,0:T(1,128)}, u32[]{:S(2)}) copy-start(f32[1,1024]{1,0:T(1,128)} %prior_ref.1) | copy-start | bytes 12292
  53.4 2.0 copy-start
  205.3 2.2 copy-start.1
Sparse Core Ops, SparseCore 0:
  55.5 149.7 all-reduce.1

commit v3 on v2

--- a/solution.py
+++ b/solution.py
@@ -64,77 +64,17 @@
     return out
 
 
-def chol_kernel(a_ref, prior_ref, ft_ref, var_ref, g_ref, linv_ref, ul_ref, ur_ref):
-    eye_r = lax.broadcasted_iota(jnp.int32, (B, N), 0)
-    eye_c = lax.broadcasted_iota(jnp.int32, (B, N), 1)
-    for i in range(NB):
-        rows = pl.ds(B * i, B)
-        g_ref[rows, :N] = a_ref[rows, :] * f32(1.0 / ROWS) + jnp.where(eye_c == eye_r + B * i, prior_ref[...], f32(0))
-        g_ref[rows, N:] = ft_ref[rows, :].astype(f32)
-    var_ref[...] = jnp.zeros_like(var_ref)
-
-    @pl.loop(0, NB)
-    def _(k):
-        k0 = pl.multiple_of(k * B, B)
-        S = [g_ref[pl.ds(k0 + 8 * i, 8), pl.ds(k0, B)] for i in range(16)]
-        out = diag_inverse(S)
-        for i in range(16):
-            linv_ref[pl.ds(8 * i, 8), :] = out[i]
-        li = linv_ref[...]
-        lh, ll = split3(li)
-        lcat = jnp.concatenate([lh, ll, lh], axis=1)
-        CW = 512
-        for c in range(W // CW):
-            gh, gl = split3(g_ref[pl.ds(k0, B), CW * c:CW * (c + 1)])
-            u = jnp.dot(lcat, jnp.concatenate([gh, gh, gl], axis=0), preferred_element_type=f32)
-            uh, ul = split3(u)
-            ur_ref[0:B, CW * c:CW * (c + 1)] = uh
-            ur_ref[B:2 * B, CW * c:CW * (c + 1)] = uh
-            ur_ref[2 * B:, CW * c:CW * (c + 1)] = ul
-            if c < N // CW:
-                for t in range(CW // B):
-                    ut = u[:, B * t:B * (t + 1)].T
-                    th, tl = split3(ut)
-                    r0 = CW * c + B * t
-                    ul_ref[r0:r0 + B, 0:B] = th
-                    ul_ref[r0:r0 + B, B:2 * B] = tl
-                    ul_ref[r0:r0 + B, 2 * B:] = th
-            else:
-                var_ref[...] += jnp.sum(u * u, axis=0, keepdims=True)
-
-        @pl.loop(k + 1, NB)
-        def _(i):
-            i0 = pl.multiple_of(i * B, B)
-            lhs = ul_ref[pl.ds(i0, B), :]
-            for c in range(W // CW):
-                d = jnp.dot(lhs, ur_ref[:, CW * c:CW * (c + 1)], preferred_element_type=f32)
-                g_ref[pl.ds(i0, B), CW * c:CW * (c + 1)] -= d
-    var_ref[...] = var_ref[...] * (4.0 / N)
-
-
-def chol_var(a, prior, ft):
-    return pl.pallas_call(
-        chol_kernel,
-        out_shape=jax.ShapeDtypeStruct((1, R_), f32),
-        in_specs=[pl.BlockSpec(memory_space=pltpu.VMEM)] * 3,
-        out_specs=pl.BlockSpec(memory_space=pltpu.VMEM),
-        scratch_shapes=[
-            pltpu.VMEM((N, W), f32),
-            pltpu.VMEM((B, B), f32),
-            pltpu.VMEM((N, 3 * B), bf16),
-            pltpu.VMEM((3 * B, W), bf16),
-        ],
-        compiler_params=pltpu.CompilerParams(vmem_limit_bytes=48 * 1024 * 1024),
-    )(a, prior, ft)
-
-
 MESH = pl.DeviceIdType.MESH
 C = 14
+MEMBERS = 8
 KB = 256
 
 
-def gather_kernel(hid_ref, proj_ref, hw_ref, hb_ref, lab_ref, cw_ref, ft_ref, gram_ref, log_ref,
-                  h_ref, buf_ref, acc_ref, wt_ref, loc_sem, send_sem, recv_sem):
+def laplace_kernel(hid_ref, proj_ref, hw_ref, hb_ref, prior_ref, lab_ref, cw_ref, var_ref, ens_ref,
+                   h_ref, buf_ref, acc_ref, ft_ref, wt_ref, gp_ref, mate_ref, part_ref, a_ref,
+                   g_ref, linv_ref, ul_ref, ur_ref, mod_ref, got_ref,
+                   loc_sem, send_sem, recv_sem, ms_sem, mr_sem, ss_sem, sr_sem, gs_sem, gr_sem, fs_sem, fr_sem,
+                   es_sem, er_sem):
     m = lax.axis_index("member")
     d = lax.axis_index("dp")
     c = lax.rem(d, 2)
@@ -153,9 +93,14 @@
     hid_copy = pltpu.make_async_copy(hid_ref, h_ref, loc_sem.at[1])
     hid_copy.start()
     bar = pltpu.get_barrier_semaphore()
-    for t in (to_r, to_l, to_y, to_m):
+    chip = d // 2
+    peers = [lax.rem(chip + rel, 8) * 2 + c for rel in range(1, 8)]
+    for t in peers + [to_m]:
         pl.semaphore_signal(bar, inc=1, device_id=(m, t), device_id_type=MESH)
-    pl.semaphore_wait(bar, 4)
+    members = [lax.rem(m + rel, MEMBERS) for rel in range(1, MEMBERS)]
+    for t in members:
+        pl.semaphore_signal(bar, inc=1, device_id=(t, d), device_id_type=MESH)
+    pl.semaphore_wait(bar, 15)
     own_copy.wait()
     sends = []
 
@@ -253,7 +198,6 @@
     for j in range(NB):
         ft_ref[B * j:B * (j + 1), :] = acc_ref[:, B * j:B * (j + 1)].T.astype(bf16)
     logits = jnp.dot(hw_ref[...], ft_ref[...], preferred_element_type=f32) + hb_ref[...]
-    log_ref[...] = logits
     cat = lax.broadcasted_iota(jnp.int32, (C, R_), 0)
     row_weight = jnp.sum(jnp.where(cat == lab_ref[...], cw_ref[...].astype(f32), f32(0)), axis=0, keepdims=True)
     expo = jnp.exp(logits)
@@ -262,50 +206,223 @@
     root = jnp.sqrt(curv)
     for j in range(NB):
         wt_ref[B * j:B * (j + 1), :] = (ft_ref[B * j:B * (j + 1), :].astype(f32) * root).astype(bf16)
-    for i in range(4):
-        gram_ref[256 * i:256 * (i + 1), 256 * i:] = lax.dot_general(
-            wt_ref[256 * i:256 * (i + 1), :], wt_ref[256 * i:, :], (((1,), (1,)), ((), ())), preferred_element_type=f32)
+
+    H = B // 2
+    mine = pl.multiple_of(c * H, H)
+    other = pl.multiple_of((1 - c) * H, H)
+
+    def mate_copy(i):
+        return pltpu.make_async_remote_copy(
+            src_ref=gp_ref.at[pl.ds(B * i + other, H), pl.ds(B * i, N - B * i)],
+            dst_ref=mate_ref.at[i, :, pl.ds(B * i, N - B * i)],
+            send_sem=ms_sem.at[i], recv_sem=mr_sem.at[i], device_id=(m, to_m), device_id_type=MESH)
+
+    def part_copy(i, rel):
+        to = lax.rem(chip + rel, 8)
+        return pltpu.make_async_remote_copy(
+            src_ref=gp_ref.at[pl.ds(pl.multiple_of(B * i + mine + 8 * to, 8), 8), pl.ds(B * i, N - B * i)],
+            dst_ref=part_ref.at[i, pl.ds(8 * (rel - 1), 8), pl.ds(B * i, N - B * i)],
+            send_sem=ss_sem.at[i], recv_sem=sr_sem.at[i], device_id=(m, to * 2 + c), device_id_type=MESH)
+
+    def part_all(i):
+        ref = part_ref.at[i, :, pl.ds(B * i, N - B * i)]
+        return pltpu.make_async_remote_copy(
+            src_ref=ref, dst_ref=ref, send_sem=ss_sem.at[i], recv_sem=sr_sem.at[i], device_id=(m, to_m), device_id_type=MESH)
+
+    def row_copy(i, rel):
+        ref = a_ref.at[pl.ds(pl.multiple_of(B * i + mine + 8 * chip, 8), 8), pl.ds(B * i, N - B * i)]
+        return pltpu.make_async_remote_copy(
+            src_ref=ref, dst_ref=ref, send_sem=gs_sem.at[i], recv_sem=gr_sem.at[i],
+            device_id=(m, lax.rem(chip + rel, 8) * 2 + c), device_id_type=MESH)
+
+    def row_all(i):
+        ref = a_ref.at[pl.ds(pl.multiple_of(B * i + mine, 8), H - 8), pl.ds(B * i, N - B * i)]
+        return pltpu.make_async_remote_copy(
+            src_ref=ref, dst_ref=ref, send_sem=gs_sem.at[i], recv_sem=gr_sem.at[i], device_id=(m, to_m), device_id_type=MESH)
+
+    def forward_copy(i):
+        ref = a_ref.at[pl.ds(pl.multiple_of(B * i + mine, H), H), pl.ds(B * i, N - B * i)]
+        return pltpu.make_async_remote_copy(
+            src_ref=ref, dst_ref=ref, send_sem=fs_sem.at[i], recv_sem=fr_sem.at[i], device_id=(m, to_m), device_id_type=MESH)
+
+    def scatter(i):
+        mate_copy(i).wait_recv()
+        rows = pl.ds(pl.multiple_of(B * i + mine, H), H)
+        gp_ref[rows, B * i:] += mate_ref[i, :, B * i:]
+        for rel in range(1, 8):
+            part_copy(i, rel).start()
+
+    def reduce(i):
+        part_all(i).wait_recv()
+        rows = pl.ds(pl.multiple_of(B * i + mine + 8 * chip, 8), 8)
+        total = gp_ref[rows, B * i:]
+        for rel in range(1, 8):
+            total += part_ref[i, 8 * (rel - 1):8 * rel, B * i:]
+        a_ref[rows, B * i:] = total
+        for rel in range(1, 8):
+            row_copy(i, rel).start()
+
+    def forward(i):
+        row_all(i).wait_recv()
+        forward_copy(i).start()
+
+    for i in range(NB):
+        gp_ref[B * i:B * (i + 1), B * i:] = lax.dot_general(
+            wt_ref[B * i:B * (i + 1), :], wt_ref[B * i:, :], (((1,), (1,)), ((), ())), preferred_element_type=f32)
+        mate_copy(i).start()
+    scatter(0)
+    for i in range(NB):
+        g_ref[B * i:B * (i + 1), :N] = jnp.zeros((B, N), f32)
+        g_ref[B * i:B * (i + 1), N:] = ft_ref[B * i:B * (i + 1), :].astype(f32)
+    reduce(0)
+    scatter(1)
+    scatter(2)
+    forward(0)
+    var_ref[...] = jnp.zeros_like(var_ref)
+    diag_r = lax.broadcasted_iota(jnp.int32, (8, B), 0)
+    diag_c = lax.broadcasted_iota(jnp.int32, (8, B), 1)
+    CW = 512
+
+    @pl.loop(0, NB)
+    def _(k):
+        k0 = pl.multiple_of(k * B, B)
+        for i in range(NB):
+            @pl.when(k == i)
+            def _(i=i):
+                forward_copy(i).wait_recv()
+                if i + 1 < NB:
+                    reduce(i + 1)
+                if i + 3 < NB:
+                    scatter(i + 3)
+        pr = prior_ref[:, pl.ds(k0, B)]
+        S = []
+        for i in range(16):
+            rows = pl.ds(k0 + 8 * i, 8)
+            s = g_ref[rows, pl.ds(k0, B)] + a_ref[rows, pl.ds(k0, B)] * f32(1.0 / ROWS)
+            S.append(s + jnp.where(diag_c == diag_r + 8 * i, pr, f32(0)))
+        out = diag_inverse(S)
+        for i in range(16):
+            linv_ref[pl.ds(8 * i, 8), :] = out[i]
+        for i in range(NB - 1):
+            @pl.when(k == i)
+            def _(i=i):
+                forward(i + 1)
+        lh, ll = split3(linv_ref[...])
+        lcat = jnp.concatenate([lh, ll, lh], axis=1)
+
+        def row_panel(c0, with_a):
+            g = g_ref[pl.ds(k0, B), c0:c0 + CW]
+            if with_a:
+                g = g + a_ref[pl.ds(k0, B), c0:c0 + CW] * f32(1.0 / ROWS)
+            gh, gl = split3(g)
+            u = jnp.dot(lcat, jnp.concatenate([gh, gh, gl], axis=0), preferred_element_type=f32)
+            uh, ul = split3(u)
+            ur_ref[0:B, c0:c0 + CW] = uh
+            ur_ref[B:2 * B, c0:c0 + CW] = uh
+            ur_ref[2 * B:, c0:c0 + CW] = ul
+            if with_a:
+                for t in range(CW // B):
+                    th, tl = split3(u[:, B * t:B * (t + 1)].T)
+                    r0 = c0 + B * t
+                    ul_ref[r0:r0 + B, 0:B] = th
+                    ul_ref[r0:r0 + B, B:2 * B] = tl
+                    ul_ref[r0:r0 + B, 2 * B:] = th
+            else:
+                var_ref[...] += jnp.sum(u * u, axis=0, keepdims=True)
+
+        row_panel(N, False)
+
+        @pl.when(k < NB - 1)
+        def _():
+            row_panel(CW, True)
+
+        @pl.when(k < NB // 2 - 1)
+        def _():
+            row_panel(0, True)
+
+        @pl.loop(k + 1, NB)
+        def _(i):
+            i0 = pl.multiple_of(i * B, B)
+            lhs = ul_ref[pl.ds(i0, B), :]
+
+            def update(c0):
+                g_ref[pl.ds(i0, B), c0:c0 + CW] -= jnp.dot(lhs, ur_ref[:, c0:c0 + CW], preferred_element_type=f32)
+
+            update(N)
+            update(CW)
+
+            @pl.when(i < NB // 2)
+            def _():
+                update(0)
+
+    var = var_ref[...] * (4.0 / P_SIZE)
+    var_ref[...] = var
+    moder = jnp.exp(logits / jnp.sqrt(1.0 + var))
+    moder = moder / jnp.sum(moder, axis=0, keepdims=True)
+    mod_ref[0:C, :] = moder
+
+    def member_copy(rel):
+        return pltpu.make_async_remote_copy(
+            src_ref=mod_ref, dst_ref=got_ref.at[rel - 1], send_sem=es_sem, recv_sem=er_sem,
+            device_id=(members[rel - 1], d), device_id_type=MESH)
+
+    for rel in range(1, MEMBERS):
+        member_copy(rel).start()
+    for i in range(NB):
+        mate_copy(i).wait_send()
+        part_all(i).wait_send()
+        row_all(i).wait_send()
+        forward_copy(i).wait_send()
+    every = pltpu.make_async_remote_copy(
+        src_ref=got_ref, dst_ref=got_ref, send_sem=es_sem, recv_sem=er_sem, device_id=(m, to_m), device_id_type=MESH)
+    every.wait_recv()
+    total = moder
+    for rel in range(1, MEMBERS):
+        total += got_ref[rel - 1, 0:C, :]
+    ens_ref[...] = total * f32(1.0 / MEMBERS)
+    every.wait_send()
     for cp in sends:
         cp.wait_send()
 
 
-def gather_features(hidden, proj, hw, hb, labels, cw):
+def laplace(hidden, proj, hw, hb, prior, labels, cw):
     vm = pl.BlockSpec(memory_space=pltpu.VMEM)
     any_ = pl.BlockSpec(memory_space=pl.ANY)
+    dma = pltpu.SemaphoreType.DMA
     return pl.pallas_call(
-        gather_kernel,
-        out_shape=(
-            jax.ShapeDtypeStruct((N, R_), bf16),
-            jax.ShapeDtypeStruct((N, N), f32),
-            jax.ShapeDtypeStruct((C, R_), f32),
-        ),
-        in_specs=[any_, any_, vm, vm, vm, vm],
-        out_specs=(vm, vm, vm),
+        laplace_kernel,
+        out_shape=(jax.ShapeDtypeStruct((1, R_), f32), jax.ShapeDtypeStruct((C, R_), f32)),
+        in_specs=[any_, any_, vm, vm, vm, vm, vm],
+        out_specs=(vm, vm),
         scratch_shapes=[
             pltpu.VMEM((R_, 4096), bf16),
             pltpu.VMEM((16, KB, P_SIZE), bf16),
             pltpu.VMEM((R_, P_SIZE), f32),
             pltpu.VMEM((N, R_), bf16),
-            pltpu.SemaphoreType.DMA((2,)),
-            pltpu.SemaphoreType.DMA((30,)),
-            pltpu.SemaphoreType.DMA((16, 2)),
+            pltpu.VMEM((N, R_), bf16),
+            pltpu.VMEM((N, N), f32),
+            pltpu.VMEM((NB, B // 2, N), f32),
+            pltpu.VMEM((NB, 56, N), f32),
+            pltpu.VMEM((N, N), f32),
+            pltpu.VMEM((N, W), f32),
+            pltpu.VMEM((B, B), f32),
+            pltpu.VMEM((N, 3 * B), bf16),
+            pltpu.VMEM((3 * B, W), bf16),
+            pltpu.VMEM((16, R_), f32),
+            pltpu.VMEM((MEMBERS - 1, 16, R_), f32),
+            dma((2,)), dma((30,)), dma((16, 2)),
+            dma((NB,)), dma((NB,)), dma((NB,)), dma((NB,)), dma((NB,)), dma((NB,)), dma((NB,)), dma((NB,)),
+            dma, dma,
         ],
         compiler_params=pltpu.CompilerParams(
-            collective_id=0, has_side_effects=True, vmem_limit_bytes=48 * 1024 * 1024),
-    )(hidden, proj, hw, hb, labels, cw)
+            collective_id=0, has_side_effects=True, vmem_limit_bytes=56 * 1024 * 1024),
+    )(hidden, proj, hw, hb, prior, labels, cw)
 
 
 def body(hidden, projection, head_weight, head_bias, prior_precision, labels, category_weight):
-    ft, gram_part, logits = gather_features(
-        hidden[0], projection[0], head_weight[0], head_bias[0][:, None], labels[None, :], category_weight[:, None])
-    gram = lax.psum(gram_part, "dp")
-    variance = chol_var(gram, prior_precision, ft)[0]
-    scaled = logits / jnp.sqrt(1.0 + variance)[None, :]
-    moder = jnp.exp(scaled)
-    moder = moder / jnp.sum(moder, axis=0, keepdims=True)
-    summed = lax.psum(moder, "member")
-    ensemble = summed / lax.axis_size("member")
-    return (variance[None, :], ensemble)
+    return laplace(
+        hidden[0], projection[0], head_weight[0], head_bias[0][:, None], prior_precision,
+        labels[None, :], category_weight[:, None])
 
 
 def solution(mesh):

time: 297 us -> 133 us (0.45)
  waiting for transfers between devices: 150 us -> 0 us
  Pallas kernels: 89.1 us -> 126 us
  blocking collectives: 33.6 us -> 0 us
  between operations: 14.1 us -> 0.64 us
    psum x1 -> x0, waiting for transfers between devices: 150 us -> none  [body(): gram = lax.psum(gram_part, 'dp')]
    pallas_call x2 -> x1, Pallas kernels: 89.1 us -> 126 us  [laplace(): pl.pallas_call(laplace_kernel, out_shape=(jax.ShapeDtypeStruct((1, R_), f...]
    psum x1 -> x0, blocking collectives: 33.6 us -> none  [body(): summed = lax.psum(moder, 'member')]
    unnamed x12 -> x2, local copies, waits for them, and re-layouts: 6.62 us -> 2.61 us
  transfers between devices with their start and end apart: 1 -> 0, of which waited for: 1 -> 0; matrix products, arithmetic and copies ran while one was open for 0% -> 0% of each run, Pallas kernels for 0% -> 0%
where the time goes in v3:
time: 133 us; the launch traced here: 131 us
  Pallas kernels  126 us (95%)
  local copies, waits for them, and re-layouts  5.28 us (4%)
    pallas_call x1, Pallas kernels, laplace(): pl.pallas_call(laplace_kernel, out_shape=(jax.ShapeDtypeStruct((1, R_), f...  126 us

profile of v3, /device:TPU:0, one launch (start us, length us, event | category | flops | bytes accessed | tf_op | source)
XLA Modules:
  0.0 131.5 jit_solution(615119737136734582)
XLA Ops:
  0.6 1.3 %copy.9.hb_ref = f32[14,1]{1,0:T(8,128)} copy(f32[14,1]{0,1:T(1,128)} %bitcast.10) | data formatting | bytes 112 | tf_op jit(solution)/shard_map/broadcast_in_dim;squeeze | solution.py:424
  2.0 1.3 %copy.10.cw_ref = s32[14,1]{1,0:T(8,128)} copy(s32[14,1]{0,1:T(1,128)} %bitcast.11) | data formatting | bytes 112 | tf_op jit(solution)/shard_map/broadcast_in_dim | solution.py:425
  3.3 125.6 %shard_map.86 = (f32[1,512]{1,0:T(1,128)}, f32[14,512]{1,0:T(8,128)}) custom-call(bf16[512,4096]{1,0:T(8,128)(2,1)} %bitcast.6, bf16[256,1024]{1,0:T(8,128)(2,1)} %bitcast.7, bf16[14,1024]{1,0:T(8,128)(2,1)} %bitcast.8, f32[14,1]{1,0:T(8,128)} %copy.9.hb_ref, f32[1,1024]{1,0:T(1,128)} %prior_ref.1, s32[1,512]{1,0:T(1,128)} %bitcast.9, s32[14,1]{1,0:T(8,128)} %copy.10.cw_ref), custom_call_target="tpu_custom_call" | custom-call | tf_op jit(solution)/shard_map/pallas_call | solution.py:392
  128.9 1.2 copy.13
  130.1 1.4 %copy.14 = f32[14,512]{1,0:T(8,128)} copy(f32[14,512]{1,0:T(8,128)} %get-tuple-element.5) | data formatting | bytes 57344

commit v4 on v3

v4 whole, which is shorter than its diff:
```python
import jax, jax.numpy as jnp
from jax import lax
from jax.experimental import pallas as pl
from jax.experimental.pallas import tpu as pltpu
from jax.sharding import PartitionSpec as P

N = 1024
P_SIZE = 1024
ROWS = 8192
B = 128
NB = N // B
R_ = 512
W = N + R_
f32 = jnp.float32
bf16 = jnp.bfloat16


def split3(x):
    hi = x.astype(bf16)
    lo = (x - hi.astype(f32)).astype(bf16)
    return hi, lo


def diag_inverse(S):
    G = 8
    n = B // G
    T = list(S)
    lane = lax.broadcasted_iota(jnp.int32, (G, B), 1)
    sub = lax.broadcasted_iota(jnp.int32, (G, B), 0)
    out = [None] * n

    def column(t, j):
        return jnp.take_along_axis(t, jnp.full((G, B), j, jnp.int32), axis=1)

    def row(t, j):
        return jnp.broadcast_to(t[j:j + 1, :], (G, B))

    for b in range(n):
        cb = [column(T[b], G * b + k) for k in range(G)]
        below = range(b + 1, n)
        cn = {i: [column(T[i], G * b + k) for k in range(G)] for i in below}
        own = (lane >= G * b) & (lane < G * b + G)
        tn = {i: jnp.where(own, f32(0), T[i]) for i in below}
        rb = T[b]
        qb = jnp.where(lane < G * b, rb, jnp.where(lane == sub + G * b, f32(1), f32(0)))
        dv = jnp.ones((G, B), f32)
        for j in range(G):
            p = row(cb[j], j)
            inv = 1.0 / p
            dv = jnp.where(sub == j, p, dv)
            m = jnp.where(sub > j, cb[j] * inv, f32(0))
            mn = {i: cn[i][j] * inv for i in below}
            for k in range(j + 1, G):
                r = row(cb[k], j)
                cb[k] = cb[k] - m * r
                for i in below:
                    cn[i][k] = cn[i][k] - mn[i] * r
            q = row(qb, j)
            if b < n - 1:
                r = row(rb, j)
                full = jnp.where(lane < G * b + G, q, r)
                for i in below:
                    tn[i] = tn[i] - mn[i] * full
                if j < G - 1:
                    rb = rb - m * r
            if j < G - 1:
                qb = qb - m * q
        out[b] = qb * lax.rsqrt(dv)
        for i in below:
            T[i] = tn[i]
    return out


MESH = pl.DeviceIdType.MESH
C = 14
MEMBERS = 8
GROUPS = ((0, 1, 0, 128), (0, 1, 128, 896), (1, 1, 128, 896), (2, 2, 256, 768), (4, 4, 512, 512))
KB = 256
MN = 512


def laplace_kernel(hid_ref, proj_ref, hw_ref, hb_ref, prior_ref, lab_ref, cw_ref, out_ref,
                   h_ref, buf_ref, acc_ref, ft_ref, wt_ref, gp_ref, mate_ref, part_ref, a_ref, var_ref,
                   g_ref, linv_ref, ul_ref, ur_ref, mod_ref, got_ref,
                   loc_sem, send_sem, recv_sem, ms_sem, mr_sem, ss_sem, sr_sem, gs_sem, gr_sem, fs_sem, fr_sem,
                   es_sem, er_sem):
    m = lax.axis_index("member")
    d = lax.axis_index("dp")
    c = lax.rem(d, 2)
    x = lax.rem(d // 2, 4)
    yh = d // 8

    def dp(dy, dx, t):
        yy = yh if dy == 0 else 1 - yh
        cc = c if t == 0 else 1 - c
        return (yy * 4 + lax.rem(x + dx, 4)) * 2 + cc

    to_r, to_l, to_y, to_m = dp(0, 1, 0), dp(0, 3, 0), dp(1, 0, 0), dp(0, 0, 1)
    me = d
    own_copy = pltpu.make_async_copy(proj_ref, buf_ref.at[d // 2, pl.ds(pl.multiple_of(c * KB, KB), KB), :], loc_sem.at[0])
    own_copy.start()
    hid_copy = pltpu.make_async_copy(hid_ref, h_ref, loc_sem.at[1])
    hid_copy.start()
    bar = pltpu.get_barrier_semaphore()
    chip = d // 2
    peers = [lax.rem(chip + rel, 8) * 2 + c for rel in range(1, 8)]
    for t in peers + [to_m]:
        pl.semaphore_signal(bar, inc=1, device_id=(m, t), device_id_type=MESH)
    members = [lax.rem(m + rel, MEMBERS) for rel in range(1, MEMBERS)]
    for t in members:
        pl.semaphore_signal(bar, inc=1, device_id=(t, d), device_id_type=MESH)
    pl.semaphore_wait(bar, 15)
    own_copy.wait()
    sends = []

    def half(s, h):
        return buf_ref.at[s // 2, pl.ds(pl.multiple_of(lax.rem(s, 2) * KB + h * (KB // 2), KB // 2), KB // 2), :]

    def copy(s, h, to, i):
        return pltpu.make_async_remote_copy(
            src_ref=half(s, h), dst_ref=half(s, h), send_sem=send_sem.at[i], recv_sem=recv_sem.at[s, h],
            device_id=(m, to), device_id_type=MESH)

    def send(to, s, h):
        cp = copy(s, h, to, len(sends))
        cp.start()
        sends.append(cp)

    def wait(s, h):
        copy(s, h, to_m, 0).wait_recv()

    def mm(s, first=False):
        place = s // 2
        k0 = pl.multiple_of(place * 2 * KB, 2 * KB)

        @pl.loop(0, P_SIZE // MN)
        def _(n):
            n0 = pl.multiple_of(n * MN, MN)
            r = jnp.dot(h_ref[:, pl.ds(k0, 2 * KB)], buf_ref[place, :, pl.ds(n0, MN)], preferred_element_type=f32)
            if first:
                acc_ref[:, pl.ds(n0, MN)] = r
            else:
                acc_ref[:, pl.ds(n0, MN)] += r

    left, right, anti, part = dp(0, 3, 0), dp(0, 1, 0), dp(0, 2, 0), dp(1, 0, 0)
    far_l, far_r, far_a = dp(1, 3, 0), dp(1, 1, 0), dp(1, 2, 0)

    def mate_mm(dy, dx, first=False):
        s = dp(dy, dx, 1)
        wait(s, 0)
        wait(s, 1)
        mm(s, first)

    send(to_r, me, 0)
    send(to_l, me, 1)
    send(to_y, me, 0)
    send(to_y, me, 1)
    send(to_r, me, 1)
    send(to_l, me, 0)
    send(to_m, me, 0)
    send(to_m, me, 1)
    for i in range(NB):
        g_ref[B * i:B * (i + 1), :N] = jnp.zeros((B, N), f32)
    hid_copy.wait()
    wait(left, 0)
    send(to_r, left, 0)
    send(to_y, left, 0)
    wait(right, 1)
    send(to_l, right, 1)
    send(to_y, right, 1)
    send(to_m, left, 0)
    send(to_m, right, 1)
    wait(part, 0)
    send(to_l, part, 0)
    wait(part, 1)
    send(to_r, part, 1)
    send(to_m, part, 0)
    send(to_m, part, 1)
    wait(left, 1)
    send(to_m, left, 1)
    wait(right, 0)
    send(to_m, right, 0)
    mate_mm(0, 0, True)
    mate_mm(0, 3)
    mate_mm(0, 1)
    wait(anti, 0)
    send(to_m, anti, 0)
    wait(anti, 1)
    send(to_m, anti, 1)
    wait(far_l, 0)
    send(to_r, far_l, 0)
    wait(far_r, 1)
    send(to_l, far_r, 1)
    send(to_m, far_l, 0)
    send(to_m, far_r, 1)
    mate_mm(1, 0)
    mate_mm(0, 2)
    wait(far_l, 1)
    send(to_m, far_l, 1)
    wait(far_r, 0)
    send(to_m, far_r, 0)
    mate_mm(1, 3)
    mate_mm(1, 1)
    wait(far_a, 0)
    send(to_m, far_a, 0)
    wait(far_a, 1)
    send(to_m, far_a, 1)
    mate_mm(1, 2)

    for j in range(NB):
        ft_ref[B * j:B * (j + 1), :] = acc_ref[:, B * j:B * (j + 1)].T.astype(bf16)
    eye = lax.broadcasted_iota(jnp.int32, (C, C), 0) == lax.broadcasted_iota(jnp.int32, (C, C), 1)
    bias = jnp.sum(jnp.where(eye, hb_ref[...], f32(0)), axis=1, keepdims=True)
    weight = jnp.sum(jnp.where(eye, cw_ref[...].astype(f32), f32(0)), axis=1, keepdims=True)
    logits = jnp.dot(hw_ref[...], ft_ref[...], preferred_element_type=f32) + bias
    cat = lax.broadcasted_iota(jnp.int32, (C, R_), 0)
    row_weight = jnp.sum(jnp.where(cat == lab_ref[...], weight, f32(0)), axis=0, keepdims=True)
    expo = jnp.exp(logits)
    probs = expo / jnp.sum(expo, axis=0, keepdims=True)
    curv = row_weight * (1.0 - jnp.sum(probs * probs, axis=0, keepdims=True))
    root = jnp.sqrt(curv)
    for j in range(NB):
        wt_ref[B * j:B * (j + 1), :] = (ft_ref[B * j:B * (j + 1), :].astype(f32) * root).astype(bf16)

    H = B // 2
    mine = pl.multiple_of(c * H, H)
    other = pl.multiple_of((1 - c) * H, H)
    slice_at = pl.multiple_of(mine + 8 * chip, 8)

    def remote(src, dst, sems, g, to):
        return pltpu.make_async_remote_copy(
            src_ref=src, dst_ref=dst, send_sem=sems[0].at[g], recv_sem=sems[1].at[g], device_id=(m, to), device_id_type=MESH)

    def view(ref, g, row0, rows):
        p0, count, col0, width = GROUPS[g]
        return ref.at[pl.ds(p0, count), pl.ds(row0, rows), pl.ds(col0, width)]

    def mate_copy(g):
        return remote(view(gp_ref, g, other, H), view(mate_ref, g, 0, H), (ms_sem, mr_sem), g, to_m)

    def part_copy(g, rel):
        to = lax.rem(chip + rel, 8)
        return remote(view(gp_ref, g, pl.multiple_of(mine + 8 * to, 8), 8), view(part_ref, g, 8 * (rel - 1), 8),
                      (ss_sem, sr_sem), g, to * 2 + c)

    def part_all(g):
        return remote(view(part_ref, g, 0, 56), view(part_ref, g, 0, 56), (ss_sem, sr_sem), g, to_m)

    def row_copy(g, rel):
        ref = view(a_ref, g, slice_at, 8)
        return remote(ref, ref, (gs_sem, gr_sem), g, lax.rem(chip + rel, 8) * 2 + c)

    def row_all(g):
        ref = view(a_ref, g, mine, 56)
        return remote(ref, ref, (gs_sem, gr_sem), g, to_m)

    def forward_copy(g):
        ref = view(a_ref, g, mine, H)
        return remote(ref, ref, (fs_sem, fr_sem), g, to_m)

    def scatter(g):
        p0, count, col0, width = GROUPS[g]
        mate_copy(g).wait_recv()
        for p in range(p0, p0 + count):
            gp_ref[p, pl.ds(mine, H), col0:col0 + width] += mate_ref[p, :, col0:col0 + width]
        for rel in range(1, 8):
            part_copy(g, rel).start()

    def reduce(g):
        p0, count, col0, width = GROUPS[g]
        part_all(g).wait_recv()
        for p in range(p0, p0 + count):
            total = gp_ref[p, pl.ds(slice_at, 8), col0:col0 + width]
            for rel in range(1, 8):
                total += part_ref[p, 8 * (rel - 1):8 * rel, col0:col0 + width]
            a_ref[p, pl.ds(slice_at, 8), col0:col0 + width] = total
        for rel in range(1, 8):
            row_copy(g, rel).start()

    def forward(g):
        row_all(g).wait_recv()
        forward_copy(g).start()

    for g, (p0, count, col0, width) in enumerate(GROUPS):
        for p in range(p0, p0 + count):
            gp_ref[p, :, col0:col0 + width] = lax.dot_general(
                wt_ref[B * p:B * (p + 1), :], wt_ref[col0:col0 + width, :], (((1,), (1,)), ((), ())), preferred_element_type=f32)
        mate_copy(g).start()
        if g == 1:
            scatter(0)
    scatter(1)
    reduce(0)
    for i in range(NB):
        g_ref[B * i:B * (i + 1), N:] = ft_ref[B * i:B * (i + 1), :].astype(f32)
    var_ref[...] = jnp.zeros_like(var_ref)
    forward(0)
    scatter(2)
    reduce(1)
    done = lambda g: forward_copy(g).wait_recv()
    at_start = {0: [(done, 0)], 1: [(done, 2), (reduce, 3), (scatter, 4)], 2: [(done, 3), (reduce, 4)], 3: [(forward, 4)], 4: [(done, 4)]}
    after_diag = {0: [(forward, 1), (reduce, 2), (scatter, 3)], 1: [(forward, 3)]}
    before_rows = {0: [(done, 1)]}
    after_rows = {0: [(forward, 2)]}

    def run(table, k):
        for key, steps in table.items():
            @pl.when(k == key)
            def _(steps=steps):
                for step, g in steps:
                    step(g)

    diag_r = lax.broadcasted_iota(jnp.int32, (8, B), 0)
    diag_c = lax.broadcasted_iota(jnp.int32, (8, B), 1)
    CW = 512

    @pl.loop(0, NB)
    def _(k):
        k0 = pl.multiple_of(k * B, B)
        run(at_start, k)
        pr = prior_ref[:, pl.ds(k0, B)]
        S = []
        for i in range(16):
            rows = pl.ds(k0 + 8 * i, 8)
            s = g_ref[rows, pl.ds(k0, B)] + a_ref[k, pl.ds(8 * i, 8), pl.ds(k0, B)] * f32(1.0 / ROWS)
            S.append(s + jnp.where(diag_c == diag_r + 8 * i, pr, f32(0)))
        out = diag_inverse(S)
        for i in range(16):
            linv_ref[pl.ds(8 * i, 8), :] = out[i]
        run(after_diag, k)
        lh, ll = split3(linv_ref[...])
        lcat = jnp.concatenate([lh, ll, lh], axis=1)

        def row_panel(c0, with_a):
            g = g_ref[pl.ds(k0, B), c0:c0 + CW]
            if with_a:
                g = g + a_ref[k, :, c0:c0 + CW] * f32(1.0 / ROWS)
            gh, gl = split3(g)
            u = jnp.dot(lcat, jnp.concatenate([gh, gh, gl], axis=0), preferred_element_type=f32)
            uh, ul = split3(u)
            ur_ref[0:B, c0:c0 + CW] = uh
            ur_ref[B:2 * B, c0:c0 + CW] = uh
            ur_ref[2 * B:, c0:c0 + CW] = ul
            if with_a:
                for t in range(CW // B):
                    th, tl = split3(u[:, B * t:B * (t + 1)].T)
                    r0 = c0 + B * t
                    ul_ref[r0:r0 + B, 0:B] = th
                    ul_ref[r0:r0 + B, B:2 * B] = tl
                    ul_ref[r0:r0 + B, 2 * B:] = th
            else:
                var_ref[...] += jnp.sum(u * u, axis=0, keepdims=True)

        row_panel(N, False)
        run(before_rows, k)

        @pl.when(k < NB - 1)
        def _():
            row_panel(CW, True)

        @pl.when(k < NB // 2 - 1)
        def _():
            row_panel(0, True)

        run(after_rows, k)

        @pl.loop(k + 1, NB)
        def _(i):
            i0 = pl.multiple_of(i * B, B)
            lhs = ul_ref[pl.ds(i0, B), :]

            def update(c0):
                g_ref[pl.ds(i0, B), c0:c0 + CW] -= jnp.dot(lhs, ur_ref[:, c0:c0 + CW], preferred_element_type=f32)

            update(N)
            update(CW)

            @pl.when(i < NB // 2)
            def _():
                update(0)

    var = var_ref[...] * (4.0 / P_SIZE)
    moder = jnp.exp(logits / jnp.sqrt(1.0 + var))
    moder = moder / jnp.sum(moder, axis=0, keepdims=True)
    mod_ref[0:C, :] = moder

    def member_copy(rel):
        return pltpu.make_async_remote_copy(
            src_ref=mod_ref, dst_ref=got_ref.at[rel - 1], send_sem=es_sem, recv_sem=er_sem,
            device_id=(members[rel - 1], d), device_id_type=MESH)

    for rel in range(1, MEMBERS):
        member_copy(rel).start()
    for g in range(len(GROUPS)):
        mate_copy(g).wait_send()
        part_all(g).wait_send()
        row_all(g).wait_send()
        forward_copy(g).wait_send()
    every = pltpu.make_async_remote_copy(
        src_ref=got_ref, dst_ref=got_ref, send_sem=es_sem, recv_sem=er_sem, device_id=(m, to_m), device_id_type=MESH)
    every.wait_recv()
    total = moder
    for rel in range(1, MEMBERS):
        total += got_ref[rel - 1, 0:C, :]
    out_ref[0:C, :] = total * f32(1.0 / MEMBERS)
    out_ref[C:C + 1, :] = var
    every.wait_send()
    for cp in sends:
        cp.wait_send()


def laplace(hidden, proj, hw, hb, prior, labels, cw):
    vm = pl.BlockSpec(memory_space=pltpu.VMEM)
    any_ = pl.BlockSpec(memory_space=pl.ANY)
    dma = pltpu.SemaphoreType.DMA
    return pl.pallas_call(
        laplace_kernel,
        out_shape=jax.ShapeDtypeStruct((16, R_), f32),
        in_specs=[any_, any_, vm, vm, vm, vm, vm],
        out_specs=vm,
        scratch_shapes=[
            pltpu.VMEM((R_, 4096), bf16),
            pltpu.VMEM((8, 2 * KB, P_SIZE), bf16),
            pltpu.VMEM((R_, P_SIZE), f32),
            pltpu.VMEM((N, R_), bf16),
            pltpu.VMEM((N, R_), bf16),
            pltpu.VMEM((NB, B, N), f32),
            pltpu.VMEM((NB, B // 2, N), f32),
            pltpu.VMEM((NB, 56, N), f32),
            pltpu.VMEM((NB, B, N), f32),
            pltpu.VMEM((1, R_), f32),
            pltpu.VMEM((N, W), f32),
            pltpu.VMEM((B, B), f32),
            pltpu.VMEM((N, 3 * B), bf16),
            pltpu.VMEM((3 * B, W), bf16),
            pltpu.VMEM((16, R_), f32),
            pltpu.VMEM((MEMBERS - 1, 16, R_), f32),
            dma((2,)), dma((30,)), dma((16, 2)),
            dma((5,)), dma((5,)), dma((5,)), dma((5,)), dma((5,)), dma((5,)), dma((5,)), dma((5,)),
            dma, dma,
        ],
        compiler_params=pltpu.CompilerParams(
            collective_id=0, has_side_effects=True, vmem_limit_bytes=56 * 1024 * 1024),
    )(hidden, proj, hw, hb, prior, labels, cw)


def finish_kernel(pack_ref, var_ref, ens_ref):
    ens_ref[...] = pack_ref[0:C, :]
    var_ref[...] = pack_ref[C:C + 1, :]


def body(hidden, projection, head_weight, head_bias, prior_precision, labels, category_weight):
    pack = laplace(
        hidden[0], projection[0], head_weight[0], head_bias, prior_precision, labels[None, :], category_weight[None, :])
    vm = pl.BlockSpec(memory_space=pltpu.VMEM)
    return pl.pallas_call(
        finish_kernel,
        out_shape=(jax.ShapeDtypeStruct((1, R_), f32), jax.ShapeDtypeStruct((C, R_), f32)),
        in_specs=[vm],
        out_specs=(vm, vm),
    )(pack)


def solution(mesh):
    return jax.shard_map(
        body,
        mesh=mesh,
        in_specs=(
            P("member", "dp", None),
            P("member", "dp", None),
            P("member", None, None),
            P("member", None),
            P("member", None),
            P("dp"),
            P(),
        ),
        out_specs=(P("member", "dp"), P(None, "dp")),
        check_vma=False,
    )
```

time: 133 us -> 120 us (0.902)
  Pallas kernels: 126 us -> 119 us
  local copies, waits for them, and re-layouts: 5.28 us -> 0 us
    pallas_call x1 -> x2, Pallas kernels: 126 us -> 119 us  [the longest x1 117 us: laplace(): pl.pallas_call(laplace_kernel, out_shape=jax.ShapeDtypeStruct((16, R_), f...]
    unnamed x2 -> x0, local copies, waits for them, and re-layouts: 2.61 us -> none
    another operation x1 -> x0, local copies, waits for them, and re-layouts: 1.34 us -> none  [body(): head_bias[0][:, None]]
    broadcast_in_dim x1 -> x0, local copies, waits for them, and re-layouts: 1.33 us -> none  [body(): category_weight[:, None]]
where the time goes in v4:
time: 120 us; the launch traced here: 119 us
  Pallas kernels  119 us (99%)
    pallas_call x1, Pallas kernels, laplace(): pl.pallas_call(laplace_kernel, out_shape=jax.ShapeDtypeStruct((16, R_), f...  117 us

profile of v4, /device:TPU:0, one launch (start us, length us, event | category | flops | bytes accessed | tf_op | source)
XLA Modules:
  0.0 119.4 jit_solution(9476434979253987955)
XLA Ops:
  0.6 117.4 %shard_map.86.pack_ref = f32[16,512]{1,0:T(8,128)} custom-call(bf16[512,4096]{1,0:T(8,128)(2,1)} %bitcast.5, bf16[256,1024]{1,0:T(8,128)(2,1)} %bitcast.6, bf16[14,1024]{1,0:T(8,128)(2,1)} %bitcast.7, f32[1,14]{1,0:T(1,128)} %hb_ref.1, f32[1,1024]{1,0:T(1,128)} %prior_ref.1, s32[1,512]{1,0:T(1,128)} %bitcast.8, s32[1,14]{1,0:T(1,128)} %bitcast.9), custom_call_target="tpu_custom_call" | custom-call | tf_op jit(solution)/shard_map/pallas_call | solution.py:415
  118.0 1.4 %shard_map.87 = (f32[1,512]{1,0:T(1,128)}, f32[14,512]{1,0:T(8,128)}) custom-call(f32[16,512]{1,0:T(8,128)} %shard_map.86.pack_ref), custom_call_target="tpu_custom_call" | custom-call | tf_op jit(solution)/shard_map/pallas_call | solution.py:455

commit v5 on v4

--- a/solution.py
+++ b/solution.py
@@ -21,13 +21,18 @@
     return hi, lo
 
 
-def diag_inverse(S):
+SB = 4
+NEXT = 2
+
+
+def diag_inverse(S, hook=lambda b: None):
     G = 8
     n = B // G
     T = list(S)
     lane = lax.broadcasted_iota(jnp.int32, (G, B), 1)
     sub = lax.broadcasted_iota(jnp.int32, (G, B), 0)
     out = [None] * n
+    held = []
 
     def column(t, j):
         return jnp.take_along_axis(t, jnp.full((G, B), j, jnp.int32), axis=1)
@@ -36,18 +41,23 @@
         return jnp.broadcast_to(t[j:j + 1, :], (G, B))
 
     for b in range(n):
+        hook(b)
+        first = b - b % SB
+        edge = min(first + SB + NEXT, n)
         cb = [column(T[b], G * b + k) for k in range(G)]
-        below = range(b + 1, n)
+        below = range(b + 1, edge)
         cn = {i: [column(T[i], G * b + k) for k in range(G)] for i in below}
         own = (lane >= G * b) & (lane < G * b + G)
         tn = {i: jnp.where(own, f32(0), T[i]) for i in below}
         rb = T[b]
         qb = jnp.where(lane < G * b, rb, jnp.where(lane == sub + G * b, f32(1), f32(0)))
         dv = jnp.ones((G, B), f32)
+        iv = jnp.ones((G, B), f32)
         for j in range(G):
             p = row(cb[j], j)
             inv = 1.0 / p
             dv = jnp.where(sub == j, p, dv)
+            iv = jnp.where(sub == j, inv, iv)
             m = jnp.where(sub > j, cb[j] * inv, f32(0))
             mn = {i: cn[i][j] * inv for i in below}
             for k in range(j + 1, G):
@@ -68,14 +78,42 @@
         out[b] = qb * lax.rsqrt(dv)
         for i in below:
             T[i] = tn[i]
+        if edge < n:
+            end = G * (first + SB)
+            held.append((rb * iv, jnp.where(lane < G * b + G, qb, jnp.where(lane < end, f32(0), rb))))
+            if b == first + SB - 1:
+                left = jnp.concatenate([x for x, _ in held], axis=0)
+                right = jnp.concatenate([y for _, y in held], axis=0)
+                lh, ll = split3(left)
+                rh, rl = split3(right)
+                prod = lax.dot_general(
+                    jnp.concatenate([lh, lh, ll], axis=0), jnp.concatenate([rh, rl, rh], axis=0),
+                    (((0,), (0,)), ((), ())), preferred_element_type=f32)
+                region = (lane >= G * first) & (lane < end)
+                for i in range(edge, n):
+                    T[i] = jnp.where(region, f32(0), T[i]) - prod[G * i:G * i + G, :]
+                held = []
     return out
 
 
 MESH = pl.DeviceIdType.MESH
 C = 14
 MEMBERS = 8
-GROUPS = ((0, 1, 0, 128), (0, 1, 128, 896), (1, 1, 128, 896), (2, 2, 256, 768), (4, 4, 512, 512))
+GROUPS = (
+    (0, 1, 0, 128),
+    (0, 1, 128, 896),
+    (1, 1, 128, 128),
+    (1, 1, 256, 768),
+    (2, 1, 256, 128),
+    (2, 1, 384, 640),
+    (3, 1, 384, 128),
+    (3, 1, 512, 512),
+    (4, 1, 512, 512),
+    (5, 1, 640, 384),
+    (6, 2, 768, 256),
+)
 KB = 256
+SLAB = 6 * B
 MN = 512
 
 
@@ -288,19 +326,29 @@
         mate_copy(g).start()
         if g == 1:
             scatter(0)
+    done = lambda g: forward_copy(g).wait_recv()
     scatter(1)
     reduce(0)
     for i in range(NB):
         g_ref[B * i:B * (i + 1), N:] = ft_ref[B * i:B * (i + 1), :].astype(f32)
     var_ref[...] = jnp.zeros_like(var_ref)
+    ul_ref[...] = jnp.zeros_like(ul_ref)
+    ur_ref[...] = jnp.zeros_like(ur_ref)
+    scatter(2)
+    scatter(3)
     forward(0)
-    scatter(2)
     reduce(1)
-    done = lambda g: forward_copy(g).wait_recv()
-    at_start = {0: [(done, 0)], 1: [(done, 2), (reduce, 3), (scatter, 4)], 2: [(done, 3), (reduce, 4)], 3: [(forward, 4)], 4: [(done, 4)]}
-    after_diag = {0: [(forward, 1), (reduce, 2), (scatter, 3)], 1: [(forward, 3)]}
-    before_rows = {0: [(done, 1)]}
-    after_rows = {0: [(forward, 2)]}
+    done(0)
+    at_start = {1: [(forward, 1)], 2: [(scatter, 10)], 3: [(reduce, 10)]}
+    before_rows = {1: [(done, 1), (forward, 2), (reduce, 4), (scatter, 6), (reduce, 5)], 2: [(done, 3)], 3: [(done, 5)], 4: [(done, 7)]}
+    before_block = {0: [(reduce, 2)], 1: [(done, 2), (scatter, 7)], 2: [(done, 4), (reduce, 7), (forward, 6)], 3: [(done, 6)], 4: [(done, 8), (forward, 10)], 5: [(done, 9)], 6: [(done, 10)]}
+    middle = {
+        2: {3: [(forward, 7)]},
+        5: {0: [(scatter, 4), (scatter, 5), (reduce, 3)], 1: [(forward, 3)]},
+        8: {1: [(forward, 4), (reduce, 6), (scatter, 8)], 2: [(reduce, 8)], 3: [(forward, 8)]},
+        11: {2: [(reduce, 9)]},
+        14: {1: [(scatter, 9), (forward, 5)], 3: [(forward, 9)]},
+    }
 
     def run(table, k):
         for key, steps in table.items():
@@ -313,71 +361,71 @@
     diag_c = lax.broadcasted_iota(jnp.int32, (8, B), 1)
     CW = 512
 
+    def row_panel(p, c0, with_a, lcat):
+        g = g_ref[pl.ds(pl.multiple_of(p * B, B), B), c0:c0 + CW]
+        if with_a:
+            g = g + a_ref[p, :, c0:c0 + CW] * f32(1.0 / ROWS)
+        gh, gl = split3(g)
+        u = jnp.dot(lcat, jnp.concatenate([gh, gh, gl], axis=0), preferred_element_type=f32)
+        uh, ul = split3(u)
+        ur_ref[0:B, c0:c0 + CW] = uh
+        ur_ref[B:2 * B, c0:c0 + CW] = uh
+        ur_ref[2 * B:, c0:c0 + CW] = ul
+        if with_a:
+            for t in range(CW // B):
+                th, tl = split3(u[:, B * t:B * (t + 1)].T)
+                r0 = c0 + B * t
+                ul_ref[r0:r0 + B, 0:B] = th
+                ul_ref[r0:r0 + B, B:2 * B] = tl
+                ul_ref[r0:r0 + B, 2 * B:] = th
+        else:
+            var_ref[...] += jnp.sum(u * u, axis=0, keepdims=True)
+
+    def inverse_factor():
+        lh, ll = split3(linv_ref[...])
+        return jnp.concatenate([lh, ll, lh], axis=1)
+
     @pl.loop(0, NB)
     def _(k):
         k0 = pl.multiple_of(k * B, B)
         run(at_start, k)
+
+        @pl.when(k > 0)
+        def _():
+            lcat = inverse_factor()
+            row_panel(k - 1, N, False, lcat)
+            run(before_rows, k)
+            row_panel(k - 1, CW, True, lcat)
+
+            @pl.when(k < NB // 2)
+            def _():
+                row_panel(k - 1, 0, True, lcat)
+            lhs = ul_ref[pl.ds(k0, B), :]
+            for c0 in (CW, N):
+                g_ref[pl.ds(k0, B), c0:c0 + CW] -= jnp.dot(lhs, ur_ref[:, c0:c0 + CW], preferred_element_type=f32)
+
+            @pl.when(k < NB // 2)
+            def _():
+                g_ref[pl.ds(k0, B), 0:CW] -= jnp.dot(lhs, ur_ref[:, 0:CW], preferred_element_type=f32)
+        run(before_block, k)
         pr = prior_ref[:, pl.ds(k0, B)]
         S = []
         for i in range(16):
-            rows = pl.ds(k0 + 8 * i, 8)
-            s = g_ref[rows, pl.ds(k0, B)] + a_ref[k, pl.ds(8 * i, 8), pl.ds(k0, B)] * f32(1.0 / ROWS)
+            s = g_ref[pl.ds(k0 + 8 * i, 8), pl.ds(k0, B)] + a_ref[k, pl.ds(8 * i, 8), pl.ds(k0, B)] * f32(1.0 / ROWS)
             S.append(s + jnp.where(diag_c == diag_r + 8 * i, pr, f32(0)))
-        out = diag_inverse(S)
+        rows = pl.ds(pl.multiple_of(k0 + B, B), SLAB)
+
+        def hook(b):
+            if b in middle:
+                run(middle[b], k)
+            if b % 2 == 1 and b // 2 < W // 256:
+                cols = slice(b // 2 * 256, (b // 2 + 1) * 256)
+                g_ref[rows, cols] -= jnp.dot(ul_ref[rows, :], ur_ref[:, cols], preferred_element_type=f32)
+        out = diag_inverse(S, hook)
         for i in range(16):
             linv_ref[pl.ds(8 * i, 8), :] = out[i]
-        run(after_diag, k)
-        lh, ll = split3(linv_ref[...])
-        lcat = jnp.concatenate([lh, ll, lh], axis=1)
-
-        def row_panel(c0, with_a):
-            g = g_ref[pl.ds(k0, B), c0:c0 + CW]
-            if with_a:
-                g = g + a_ref[k, :, c0:c0 + CW] * f32(1.0 / ROWS)
-            gh, gl = split3(g)
-            u = jnp.dot(lcat, jnp.concatenate([gh, gh, gl], axis=0), preferred_element_type=f32)
-            uh, ul = split3(u)
-            ur_ref[0:B, c0:c0 + CW] = uh
-            ur_ref[B:2 * B, c0:c0 + CW] = uh
-            ur_ref[2 * B:, c0:c0 + CW] = ul
-            if with_a:
-                for t in range(CW // B):
-                    th, tl = split3(u[:, B * t:B * (t + 1)].T)
-                    r0 = c0 + B * t
-                    ul_ref[r0:r0 + B, 0:B] = th
-                    ul_ref[r0:r0 + B, B:2 * B] = tl
-                    ul_ref[r0:r0 + B, 2 * B:] = th
-            else:
-                var_ref[...] += jnp.sum(u * u, axis=0, keepdims=True)
-
-        row_panel(N, False)
-        run(before_rows, k)
-
-        @pl.when(k < NB - 1)
-        def _():
-            row_panel(CW, True)
-
-        @pl.when(k < NB // 2 - 1)
-        def _():
-            row_panel(0, True)
-
-        run(after_rows, k)
-
-        @pl.loop(k + 1, NB)
-        def _(i):
-            i0 = pl.multiple_of(i * B, B)
-            lhs = ul_ref[pl.ds(i0, B), :]
-
-            def update(c0):
-                g_ref[pl.ds(i0, B), c0:c0 + CW] -= jnp.dot(lhs, ur_ref[:, c0:c0 + CW], preferred_element_type=f32)
-
-            update(N)
-            update(CW)
-
-            @pl.when(i < NB // 2)
-            def _():
-                update(0)
-
+
+    row_panel(NB - 1, N, False, inverse_factor())
     var = var_ref[...] * (4.0 / P_SIZE)
     moder = jnp.exp(logits / jnp.sqrt(1.0 + var))
     moder = moder / jnp.sum(moder, axis=0, keepdims=True)
@@ -428,14 +476,14 @@
             pltpu.VMEM((NB, 56, N), f32),
             pltpu.VMEM((NB, B, N), f32),
             pltpu.VMEM((1, R_), f32),
-            pltpu.VMEM((N, W), f32),
+            pltpu.VMEM((N + SLAB, W), f32),
             pltpu.VMEM((B, B), f32),
-            pltpu.VMEM((N, 3 * B), bf16),
+            pltpu.VMEM((N + SLAB, 3 * B), bf16),
             pltpu.VMEM((3 * B, W), bf16),
             pltpu.VMEM((16, R_), f32),
             pltpu.VMEM((MEMBERS - 1, 16, R_), f32),
             dma((2,)), dma((30,)), dma((16, 2)),
-            dma((5,)), dma((5,)), dma((5,)), dma((5,)), dma((5,)), dma((5,)), dma((5,)), dma((5,)),
+            dma((11,)), dma((11,)), dma((11,)), dma((11,)), dma((11,)), dma((11,)), dma((11,)), dma((11,)),
             dma, dma,
         ],
         compiler_params=pltpu.CompilerParams(

time: 120 us -> 107 us (0.89)
  Pallas kernels: 119 us -> 106 us
    pallas_call x1, Pallas kernels: 117 us -> 104 us  [laplace(): pl.pallas_call(laplace_kernel, out_shape=jax.ShapeDtypeStruct((16, R_), f...]
where the time goes in v5:
time: 107 us
  Pallas kernels  106 us (99%)
    pallas_call x1, Pallas kernels, laplace(): pl.pallas_call(laplace_kernel, out_shape=jax.ShapeDtypeStruct((16, R_), f...  104 us

profile of v5, /device:TPU:0, one launch (start us, length us, event | category | flops | bytes accessed | tf_op | source)
XLA Modules:
  0.0 106.5 jit_solution(971137487857706298)
XLA Ops:
  0.6 104.5 %shard_map.86.pack_ref = f32[16,512]{1,0:T(8,128)} custom-call(bf16[512,4096]{1,0:T(8,128)(2,1)} %bitcast.5, bf16[256,1024]{1,0:T(8,128)(2,1)} %bitcast.6, bf16[14,1024]{1,0:T(8,128)(2,1)} %bitcast.7, f32[1,14]{1,0:T(1,128)} %hb_ref.1, f32[1,1024]{1,0:T(1,128)} %prior_ref.1, s32[1,512]{1,0:T(1,128)} %bitcast.8, s32[1,14]{1,0:T(1,128)} %bitcast.9), custom_call_target="tpu_custom_call" | custom-call | tf_op jit(solution)/shard_map/pallas_call | solution.py:463
  105.1 1.4 %shard_map.87 = (f32[1,512]{1,0:T(1,128)}, f32[14,512]{1,0:T(8,128)}) custom-call(f32[16,512]{1,0:T(8,128)} %shard_map.86.pack_ref), custom_call_target="tpu_custom_call" | custom-call | tf_op jit(solution)/shard_map/pallas_call | solution.py:503

commit v6 on v5

--- a/solution.py
+++ b/solution.py
@@ -22,7 +22,7 @@
 
 
 SB = 4
-NEXT = 2
+NEXT = 1
 
 
 def diag_inverse(S, hook=lambda b: None):
@@ -44,9 +44,11 @@
         hook(b)
         first = b - b % SB
         edge = min(first + SB + NEXT, n)
-        cb = [column(T[b], G * b + k) for k in range(G)]
+        cb = ahead if b else [column(T[b], G * b + k) for k in range(G)]
         below = range(b + 1, edge)
         cn = {i: [column(T[i], G * b + k) for k in range(G)] for i in below}
+        if b < n - 1:
+            ahead = [column(T[b + 1], G * (b + 1) + k) for k in range(G)]
         own = (lane >= G * b) & (lane < G * b + G)
         tn = {i: jnp.where(own, f32(0), T[i]) for i in below}
         rb = T[b]
@@ -60,6 +62,9 @@
             iv = jnp.where(sub == j, inv, iv)
             m = jnp.where(sub > j, cb[j] * inv, f32(0))
             mn = {i: cn[i][j] * inv for i in below}
+            if b < n - 1:
+                for k in range(G):
+                    ahead[k] = ahead[k] - mn[b + 1] * row(cn[b + 1][j], k)
             for k in range(j + 1, G):
                 r = row(cb[k], j)
                 cb[k] = cb[k] - m * r
@@ -104,12 +109,9 @@
     (0, 1, 128, 896),
     (1, 1, 128, 128),
     (1, 1, 256, 768),
-    (2, 1, 256, 128),
-    (2, 1, 384, 640),
-    (3, 1, 384, 128),
-    (3, 1, 512, 512),
-    (4, 1, 512, 512),
-    (5, 1, 640, 384),
+    (2, 1, 256, 768),
+    (3, 1, 384, 640),
+    (4, 2, 512, 512),
     (6, 2, 768, 256),
 )
 KB = 256
@@ -339,15 +341,13 @@
     forward(0)
     reduce(1)
     done(0)
-    at_start = {1: [(forward, 1)], 2: [(scatter, 10)], 3: [(reduce, 10)]}
-    before_rows = {1: [(done, 1), (forward, 2), (reduce, 4), (scatter, 6), (reduce, 5)], 2: [(done, 3)], 3: [(done, 5)], 4: [(done, 7)]}
-    before_block = {0: [(reduce, 2)], 1: [(done, 2), (scatter, 7)], 2: [(done, 4), (reduce, 7), (forward, 6)], 3: [(done, 6)], 4: [(done, 8), (forward, 10)], 5: [(done, 9)], 6: [(done, 10)]}
+    at_start = {3: [(forward, 5)]}
+    before_rows = {1: [(forward, 1), (done, 1), (forward, 2), (scatter, 5)], 2: [(done, 3), (reduce, 5)]}
+    before_block = {0: [(reduce, 2)], 1: [(done, 2), (reduce, 4)], 2: [(forward, 4), (done, 4), (scatter, 7)], 3: [(done, 5), (reduce, 7)], 4: [(done, 6), (forward, 7)], 6: [(done, 7)]}
     middle = {
-        2: {3: [(forward, 7)]},
-        5: {0: [(scatter, 4), (scatter, 5), (reduce, 3)], 1: [(forward, 3)]},
-        8: {1: [(forward, 4), (reduce, 6), (scatter, 8)], 2: [(reduce, 8)], 3: [(forward, 8)]},
-        11: {2: [(reduce, 9)]},
-        14: {1: [(scatter, 9), (forward, 5)], 3: [(forward, 9)]},
+        4: {0: [(scatter, 4)]},
+        8: {0: [(reduce, 3)], 1: [(forward, 3)], 2: [(reduce, 6)]},
+        12: {1: [(scatter, 6)], 3: [(forward, 6)]},
     }
 
     def run(table, k):
@@ -483,7 +483,7 @@
             pltpu.VMEM((16, R_), f32),
             pltpu.VMEM((MEMBERS - 1, 16, R_), f32),
             dma((2,)), dma((30,)), dma((16, 2)),
-            dma((11,)), dma((11,)), dma((11,)), dma((11,)), dma((11,)), dma((11,)), dma((11,)), dma((11,)),
+            dma((8,)), dma((8,)), dma((8,)), dma((8,)), dma((8,)), dma((8,)), dma((8,)), dma((8,)),
             dma, dma,
         ],
         compiler_params=pltpu.CompilerParams(

time: 107 us -> 102 us (0.953)
  Pallas kernels: 106 us -> 101 us
    pallas_call x1, Pallas kernels: 104 us -> 100 us  [laplace(): pl.pallas_call(laplace_kernel, out_shape=jax.ShapeDtypeStruct((16, R_), f...]
where the time goes in v6:
time: 102 us
  Pallas kernels  101 us (99%)
    pallas_call x1, Pallas kernels, laplace(): pl.pallas_call(laplace_kernel, out_shape=jax.ShapeDtypeStruct((16, R_), f...  100 us

profile of v6, /device:TPU:0, one launch (start us, length us, event | category | flops | bytes accessed | tf_op | source)
XLA Modules:
  0.0 102.1 jit_solution(445360991058389052)
XLA Ops:
  0.6 100.0 %shard_map.86.pack_ref = f32[16,512]{1,0:T(8,128)} custom-call(bf16[512,4096]{1,0:T(8,128)(2,1)} %bitcast.5, bf16[256,1024]{1,0:T(8,128)(2,1)} %bitcast.6, bf16[14,1024]{1,0:T(8,128)(2,1)} %bitcast.7, f32[1,14]{1,0:T(1,128)} %hb_ref.1, f32[1,1024]{1,0:T(1,128)} %prior_ref.1, s32[1,512]{1,0:T(1,128)} %bitcast.8, s32[1,14]{1,0:T(1,128)} %bitcast.9), custom_call_target="tpu_custom_call" | custom-call | tf_op jit(solution)/shard_map/pallas_call | solution.py:463
  100.7 1.4 %shard_map.87 = (f32[1,512]{1,0:T(1,128)}, f32[14,512]{1,0:T(8,128)}) custom-call(f32[16,512]{1,0:T(8,128)} %shard_map.86.pack_ref), custom_call_target="tpu_custom_call" | custom-call | tf_op jit(solution)/shard_map/pallas_call | solution.py:503

commit v7 on v6

--- a/solution.py
+++ b/solution.py
@@ -182,6 +182,16 @@
             else:
                 acc_ref[:, pl.ds(n0, MN)] += r
 
+    def mm_half(s):
+        k0 = pl.multiple_of(s * KB, KB)
+        row0 = pl.multiple_of(lax.rem(s, 2) * KB, KB)
+
+        @pl.loop(0, P_SIZE // MN)
+        def _(n):
+            n0 = pl.multiple_of(n * MN, MN)
+            acc_ref[:, pl.ds(n0, MN)] += jnp.dot(
+                h_ref[:, pl.ds(k0, KB)], buf_ref[s // 2, pl.ds(row0, KB), pl.ds(n0, MN)], preferred_element_type=f32)
+
     left, right, anti, part = dp(0, 3, 0), dp(0, 1, 0), dp(0, 2, 0), dp(1, 0, 0)
     far_l, far_r, far_a = dp(1, 3, 0), dp(1, 1, 0), dp(1, 2, 0)
 
@@ -201,6 +211,8 @@
     send(to_m, me, 1)
     for i in range(NB):
         g_ref[B * i:B * (i + 1), :N] = jnp.zeros((B, N), f32)
+    ul_ref[...] = jnp.zeros_like(ul_ref)
+    ur_ref[...] = jnp.zeros_like(ur_ref)
     hid_copy.wait()
     wait(left, 0)
     send(to_r, left, 0)
@@ -245,7 +257,11 @@
     send(to_m, far_a, 0)
     wait(far_a, 1)
     send(to_m, far_a, 1)
-    mate_mm(1, 2)
+    mm_half(far_a)
+    last = dp(1, 2, 1)
+    wait(last, 0)
+    wait(last, 1)
+    mm_half(last)
 
     for j in range(NB):
         ft_ref[B * j:B * (j + 1), :] = acc_ref[:, B * j:B * (j + 1)].T.astype(bf16)
@@ -328,14 +344,14 @@
         mate_copy(g).start()
         if g == 1:
             scatter(0)
+        if g == 4:
+            scatter(1)
+        if g == 5:
+            reduce(0)
     done = lambda g: forward_copy(g).wait_recv()
-    scatter(1)
-    reduce(0)
     for i in range(NB):
         g_ref[B * i:B * (i + 1), N:] = ft_ref[B * i:B * (i + 1), :].astype(f32)
     var_ref[...] = jnp.zeros_like(var_ref)
-    ul_ref[...] = jnp.zeros_like(ul_ref)
-    ur_ref[...] = jnp.zeros_like(ur_ref)
     scatter(2)
     scatter(3)
     forward(0)

time: 102 us -> 102 us (level)
  no operation moved by 1% of the time
where the time goes in v7:
time: 102 us
  Pallas kernels  101 us (99%)
    pallas_call x1, Pallas kernels, laplace(): pl.pallas_call(laplace_kernel, out_shape=jax.ShapeDtypeStruct((16, R_), f...  99.7 us

profile of v7, /device:TPU:0, one launch (start us, length us, event | category | flops | bytes accessed | tf_op | source)
XLA Modules:
  0.0 101.7 jit_solution(12791413279979146602)
XLA Ops:
  0.6 99.7 %shard_map.86.pack_ref = f32[16,512]{1,0:T(8,128)} custom-call(bf16[512,4096]{1,0:T(8,128)(2,1)} %bitcast.5, bf16[256,1024]{1,0:T(8,128)(2,1)} %bitcast.6, bf16[14,1024]{1,0:T(8,128)(2,1)} %bitcast.7, f32[1,14]{1,0:T(1,128)} %hb_ref.1, f32[1,1024]{1,0:T(1,128)} %prior_ref.1, s32[1,512]{1,0:T(1,128)} %bitcast.8, s32[1,14]{1,0:T(1,128)} %bitcast.9), custom_call_target="tpu_custom_call" | custom-call | tf_op jit(solution)/shard_map/pallas_call | solution.py:479
  100.3 1.4 %shard_map.87 = (f32[1,512]{1,0:T(1,128)}, f32[14,512]{1,0:T(8,128)}) custom-call(f32[16,512]{1,0:T(8,128)} %shard_map.86.pack_ref), custom_call_target="tpu_custom_call" | custom-call | tf_op jit(solution)/shard_map/pallas_call | solution.py:519

commit v8 on v7

--- a/solution.py
+++ b/solution.py
@@ -144,11 +144,11 @@
     bar = pltpu.get_barrier_semaphore()
     chip = d // 2
     peers = [lax.rem(chip + rel, 8) * 2 + c for rel in range(1, 8)]
-    for t in peers + [to_m]:
-        pl.semaphore_signal(bar, inc=1, device_id=(m, t), device_id_type=MESH)
     members = [lax.rem(m + rel, MEMBERS) for rel in range(1, MEMBERS)]
     for t in members:
         pl.semaphore_signal(bar, inc=1, device_id=(t, d), device_id_type=MESH)
+    for t in peers + [to_m]:
+        pl.semaphore_signal(bar, inc=1, device_id=(m, t), device_id_type=MESH)
     pl.semaphore_wait(bar, 15)
     own_copy.wait()
     sends = []

time: 102 us -> 102 us (level)
  no operation moved by 1% of the time
where the time goes in v8:
time: 102 us
  Pallas kernels  101 us (99%)
    pallas_call x1, Pallas kernels, laplace(): pl.pallas_call(laplace_kernel, out_shape=jax.ShapeDtypeStruct((16, R_), f...  99.7 us

profile of v8, /device:TPU:0, one launch (start us, length us, event | category | flops | bytes accessed | tf_op | source)
XLA Modules:
  0.0 101.7 jit_solution(7056084883560354230)
XLA Ops:
  0.6 99.7 %shard_map.86.pack_ref = f32[16,512]{1,0:T(8,128)} custom-call(bf16[512,4096]{1,0:T(8,128)(2,1)} %bitcast.5, bf16[256,1024]{1,0:T(8,128)(2,1)} %bitcast.6, bf16[14,1024]{1,0:T(8,128)(2,1)} %bitcast.7, f32[1,14]{1,0:T(1,128)} %hb_ref.1, f32[1,1024]{1,0:T(1,128)} %prior_ref.1, s32[1,512]{1,0:T(1,128)} %bitcast.8, s32[1,14]{1,0:T(1,128)} %bitcast.9), custom_call_target="tpu_custom_call" | custom-call | tf_op jit(solution)/shard_map/pallas_call | solution.py:479
  100.4 1.4 %shard_map.87 = (f32[1,512]{1,0:T(1,128)}, f32[14,512]{1,0:T(8,128)}) custom-call(f32[16,512]{1,0:T(8,128)} %shard_map.86.pack_ref), custom_call_target="tpu_custom_call" | custom-call | tf_op jit(solution)/shard_map/pallas_call | solution.py:519
